TPU v7x, 256 devices: a whole 4x4x8 slice. The times are simulated.
256 devices in a mesh: row: 16 (over y_hi, x, core), col: 16 (over z, y_lo).
Axes of the slice: x: 4, y: 4 (y_hi: 2, y_lo: 2; y = y_hi * 2 + y_lo), z: 8, core: 2. Of those that a mesh axis runs over, the one named last changes fastest.
Arguments:
- attn_context: bfloat16 [8192, 4096], P('row', 'col'), may hold values from -6 to 6
- residual: bfloat16 [8192, 2048], P('row', 'col'), may hold values from -8 to 8
- w_out: bfloat16 [4096, 2048], P('col'), may hold values from -0.09375 to 0.09375
- gain_post: bfloat16 [2048], replicated, may hold values from 0.5 to 1.5
- gain_input: bfloat16 [2048], replicated, may hold values from 0.5 to 1.5
- routes: int32 [8192, 8], P('row'), may hold values from 0 to 127, all different within a row; in each aligned block of 512 rows (0 to 511, 512 to 1023, ...) at most 64 rows name the same one
- router_scores: float32 [8192, 8], P('row'), may hold values from 0.02 to 1
- w_gate: bfloat16 [256, 2048, 384], P(('row', 'col')), may hold values from -0.125 to 0.125
- w_up: bfloat16 [256, 2048, 384], P(('row', 'col')), may hold values from -0.125 to 0.125
- w_down: bfloat16 [256, 384, 2048], P(('row', 'col')), may hold values from -0.21875 to 0.21875
- w_query: bfloat16 [2048, 4096], P(None, 'col'), may hold values from -1 to 1
- w_keyval: bfloat16 [2048, 1024], P(None, 'col'), may hold values from -1 to 1
- segment_ids: int32 [16, 504], P('row'), may hold values from 0 to 3, never falling along the last dimension, each value on 1 to 252 neighbouring positions
- cache_lengths: int32 [128], P('row'), may hold values from 1 to 1024, 65536 in all
- holders: int32 [128], P('row'), may hold values from 0 to 127, each once
- cache_keys: bfloat16 [128, 1024, 512], P('row', 'col'), may hold values from -12 to 12
- cache_values: bfloat16 [128, 1024, 512], P('row', 'col'), may hold values from -12 to 12
Outputs:
- hidden_out: bfloat16 [8192, 2048], P('row', 'col')
- new_cache: bfloat16 [8192, 1024], P('row', 'col')
- attention_out: bfloat16 [8192, 4096], P('row', 'col')
Inputs may be any that keep to these rules, and one draw needn't show every extreme that they name: `routes`: in the 512 rows of one index of row, no expert is named by more than 64 rows, and in every draw some expert is named by exactly 64. `segment_ids`: each prompt has at most 252 rows and one has exactly that many. `cache_lengths`: the lengths sum to 65536 and the largest is 1024. `holders`: each cache entry belongs to exactly one decode row.
All inputs are finite; a program needn't handle non-finite values. No bound on the sum of `cache_lengths` on one device may be relied on, other than what follows from the above.
Results may differ from a plain program's by a relative error of at most 0.0175.
Values may be sent and summed in bfloat16 or wider, within the bound.
A program may use at most 128 MiB of HBM per device.

v0:
```python
import jax
import jax.numpy as jnp
from jax import lax
from jax.sharding import PartitionSpec as P

TOP = 8
QH = 32
KVH = 4
HD = 128


EPSILON = 1e-06
ROPE_THETA = 1000000.0
NEGATIVE = -1e30


def merged_2(value, axis, join):
    pieces = jax.tree.map(lambda part: lax.all_gather(part, axis), value)
    head = jax.tree.map(lambda part: part[0], pieces)
    tail = jax.tree.map(lambda part: part[1:], pieces)
    running, _ = lax.scan(lambda running, share: (join(running, share), None), head, tail)
    return running


def rms_norm(hidden, gain_vector):
    values = hidden.astype(jnp.float32)
    inverse = lax.rsqrt(jnp.mean(values * values, axis=-1, keepdims=True) + EPSILON)
    return (values * inverse * gain_vector.astype(jnp.float32)).astype(jnp.bfloat16)


def rotate(values, positions):
    head_width = values.shape[-1]
    half_width = head_width // 2
    indices = jnp.arange(half_width).astype(jnp.float32)
    inverse = ROPE_THETA ** (-2.0 * indices / head_width)
    angles = positions.astype(jnp.float32)[:, None] * inverse[None, :]
    cosine = jnp.concatenate([jnp.cos(angles), jnp.cos(angles)], axis=-1)[:, None, :]
    sine_part = jnp.concatenate([jnp.sin(angles), jnp.sin(angles)], axis=-1)[:, None, :]
    floats = values.astype(jnp.float32)
    turned = jnp.concatenate([-floats[..., half_width:], floats[..., :half_width]], axis=-1)
    return (floats * cosine + turned * sine_part).astype(jnp.bfloat16)


def segment_positions(segment_rows):
    earlier = jnp.sum((segment_rows[None, :] < segment_rows[:, None]).astype(jnp.int32), axis=1)
    return jnp.arange(segment_rows.shape[0], dtype=jnp.int32) - earlier


def spread_norm(hidden, gain_vector):
    gathered = lax.all_gather(hidden, "col", axis=1, tiled=True)
    return (gathered, rms_norm(gathered, gain_vector))


def join_partials(first, second):
    highest = jnp.maximum(first[0], second[0])
    factor_one = jnp.exp(first[0] - highest)
    factor_two = jnp.exp(second[0] - highest)
    weight_mass = first[1] * factor_one + second[1] * factor_two
    accum_out = first[2] * factor_one[..., None] + second[2] * factor_two[..., None]
    return (highest, weight_mass, accum_out)


def shards(
    attn_context,
    residual,
    w_out,
    gain_post,
    gain_input,
    routes,
    router_scores,
    w_gate,
    w_up,
    w_down,
    w_query,
    w_keyval,
    segment_ids,
    cache_lengths,
    holders,
    cache_keys,
    cache_values,
):
    col_index = lax.axis_index("col")
    col_count = lax.axis_size("col")
    row_count = lax.axis_size("row")
    tok_rows = attn_context.shape[0]
    share_width = residual.shape[1]
    model_width = share_width * col_count
    projected = jnp.dot(attn_context, w_out, preferred_element_type=jnp.float32)
    summed = lax.psum_scatter(projected, "col", scatter_dimension=1, tiled=True)
    hidden_mid = (residual.astype(jnp.float32) + summed).astype(jnp.bfloat16)
    full_mid, normed = spread_norm(hidden_mid, gain_post)
    group_width = col_count // 2
    expert_count = row_count * group_width
    capacity = 2 * tok_rows * TOP // expert_count
    route_weight = router_scores / jnp.sum(router_scores, axis=1, keepdims=True)
    matching = routes % group_width == col_index // 2
    target = routes // group_width
    dest_ids = jnp.arange(row_count, dtype=jnp.int32)
    hitting = matching[:, :, None] & (target[:, :, None] == dest_ids[None, None, :])
    sent_flag = jnp.sum(hitting.astype(jnp.int32), axis=1)
    sent_weight = jnp.sum(jnp.where(hitting, route_weight[:, :, None], 0.0), axis=1)
    place = jnp.cumsum(sent_flag, axis=0) - sent_flag
    dest_or_drop = jnp.where(sent_flag > 0, dest_ids[None, :], row_count)
    row_ids = jnp.broadcast_to(
        jnp.arange(tok_rows, dtype=jnp.int32)[:, None], (tok_rows, row_count)
    )
    slot_rows = (
        jnp.full((row_count, capacity), tok_rows, jnp.int32)
        .at[dest_or_drop, place]
        .set(row_ids, mode="drop")
    )
    slot_weight = (
        jnp.zeros((row_count, capacity), jnp.float32)
        .at[dest_or_drop, place]
        .set(sent_weight, mode="drop")
    )
    padded = jnp.concatenate([normed, jnp.zeros((1, model_width), jnp.bfloat16)], axis=0)
    outgoing = padded[slot_rows]
    gate_local = w_gate[0]
    up_local = w_up[0]
    down_local = w_down[0]
    arrived = lax.all_to_all(outgoing, "row", split_axis=0, concat_axis=0, tiled=True)
    flat_rows = arrived.reshape(-1, arrived.shape[2])
    gate_part = jnp.dot(flat_rows, gate_local, preferred_element_type=jnp.float32)
    up_part = jnp.dot(flat_rows, up_local, preferred_element_type=jnp.float32)
    inner = (jax.nn.silu(gate_part) * up_part).astype(jnp.bfloat16)
    result = jnp.dot(inner, down_local, preferred_element_type=jnp.float32).astype(jnp.bfloat16)
    returned = lax.all_to_all(
        result.reshape(arrived.shape), "row", split_axis=0, concat_axis=0, tiled=True
    )
    weighted = slot_weight[:, :, None] * returned.astype(jnp.float32)
    partial_moe = (
        jnp.zeros((tok_rows, model_width), jnp.float32)
        .at[slot_rows.reshape(-1)]
        .add(weighted.reshape(-1, model_width), mode="drop")
    )
    moe_share = lax.psum_scatter(partial_moe, "col", scatter_dimension=1, tiled=True)
    hidden_out = (hidden_mid.astype(jnp.float32) + moe_share).astype(jnp.bfloat16)
    _, x_in = spread_norm(hidden_out, gain_input)
    heads_local = QH // col_count
    dec_count = cache_lengths.shape[0]
    score_scale = HD ** (-0.5)
    query_local = (
        jnp.dot(x_in, w_query, preferred_element_type=jnp.float32)
        .astype(jnp.bfloat16)
        .reshape(tok_rows, heads_local, HD)
    )
    keyval_local = jnp.dot(x_in, w_keyval, preferred_element_type=jnp.float32).astype(jnp.bfloat16)
    position = jnp.concatenate([cache_lengths, segment_positions(segment_ids[0])], axis=0)
    query_rot = rotate(query_local, position)
    dec_query = query_rot[:dec_count].reshape(dec_count, heads_local * HD)
    keyval_all, payload = (
        lax.all_gather(keyval_local, "col", axis=1, tiled=True),
        lax.all_gather(dec_query, "col", axis=1, tiled=True),
    )
    keyval_heads = keyval_all.reshape(tok_rows, KVH, 2, HD)
    key_rot = rotate(keyval_heads[:, :, 0, :], position)
    value_rows = keyval_heads[:, :, 1, :]
    cache_full = jnp.stack([key_rot, value_rows], axis=2).reshape(tok_rows, 2 * KVH * HD)
    cache_share = cache_full.shape[1] // col_count
    new_cache = lax.dynamic_slice_in_dim(cache_full, col_index * cache_share, cache_share, 1)
    head_kv = col_index * heads_local // (QH // KVH)
    my_keys = lax.dynamic_index_in_dim(key_rot, head_kv, 1, keepdims=False)
    my_values = lax.dynamic_index_in_dim(value_rows, head_kv, 1, keepdims=False)
    prompt_query = query_rot[dec_count:]
    prompt_keys = my_keys[dec_count:]
    prompt_values = my_values[dec_count:]
    prompt_rows = prompt_query.shape[0]
    scores = (
        jnp.einsum("ihd,jd->hij", prompt_query, prompt_keys, preferred_element_type=jnp.float32)
        * score_scale
    )
    ordinal = jnp.arange(prompt_rows)
    segment_rows = segment_ids[0]
    allowed = (segment_rows[:, None] == segment_rows[None, :]) & (
        ordinal[None, :] <= ordinal[:, None]
    )
    scores = jnp.where(allowed[None, :, :], scores, NEGATIVE)
    highest = jnp.max(scores, axis=-1, keepdims=True)
    exponent = jnp.exp(scores - highest)
    probability = (exponent / jnp.sum(exponent, axis=-1, keepdims=True)).astype(jnp.bfloat16)
    prompt_out = jnp.einsum(
        "hij,jd->ihd", probability, prompt_values, preferred_element_type=jnp.float32
    )
    prompt_out = prompt_out.astype(jnp.bfloat16).reshape(prompt_rows, heads_local * HD)
    holder_dev = holders // dec_count
    holder_slot = holders % dec_count
    outbox = (
        jnp.zeros((row_count, dec_count, payload.shape[1]), jnp.bfloat16)
        .at[holder_dev, holder_slot]
        .set(payload)
    )
    length_box = (
        jnp.zeros((row_count, dec_count), jnp.int32).at[holder_dev, holder_slot].set(cache_lengths)
    )
    inbox, length_in = (
        lax.all_to_all(outbox, "row", split_axis=0, concat_axis=0, tiled=True),
        lax.all_to_all(length_box, "row", split_axis=0, concat_axis=0, tiled=True),
    )
    slot_query = jnp.sum(inbox.astype(jnp.float32), axis=0).astype(jnp.bfloat16)
    slot_length = jnp.sum(length_in, axis=0)
    span_len = cache_keys.shape[1]
    span_start = col_index * span_len
    grouped = slot_query.reshape(dec_count, KVH, QH // KVH, HD)
    held_keys = cache_keys.reshape(dec_count, span_len, KVH, HD)
    held_values = cache_values.reshape(dec_count, span_len, KVH, HD).astype(jnp.float32)
    held_scores = (
        jnp.einsum("sgqd,stgd->sgqt", grouped, held_keys, preferred_element_type=jnp.float32)
        * score_scale
    )
    valid = ((span_start + jnp.arange(span_len))[None, :] < slot_length[:, None])[:, None, None, :]
    held_scores = jnp.where(valid, held_scores, NEGATIVE)
    score_top = jnp.max(held_scores, axis=-1)
    held_exp = jnp.where(valid, jnp.exp(held_scores - score_top[..., None]), 0.0)
    weight_mass = jnp.sum(held_exp, axis=-1).reshape(dec_count, QH)
    accum_out = jnp.einsum(
        "sgqt,stgd->sgqd", held_exp, held_values, precision=lax.Precision.HIGHEST
    ).reshape(dec_count, QH, HD)
    score_top = score_top.reshape(dec_count, QH)
    merged = merged_2((score_top, weight_mass, accum_out), "col", join_partials)
    part_top = lax.dynamic_slice_in_dim(merged[0], col_index * heads_local, heads_local, 1)
    part_mass = lax.dynamic_slice_in_dim(merged[1], col_index * heads_local, heads_local, 1)
    part_accum = lax.dynamic_slice_in_dim(merged[2], col_index * heads_local, heads_local, 1)
    reply_top = jnp.broadcast_to(part_top[None], (row_count,) + part_top.shape)
    reply_mass = jnp.broadcast_to(part_mass[None], (row_count,) + part_mass.shape)
    reply_accum = jnp.broadcast_to(part_accum[None], (row_count,) + part_accum.shape)
    back_top, back_mass, back_accum = (
        lax.all_to_all(reply_top, "row", split_axis=0, concat_axis=0, tiled=True),
        lax.all_to_all(reply_mass, "row", split_axis=0, concat_axis=0, tiled=True),
        lax.all_to_all(reply_accum, "row", split_axis=0, concat_axis=0, tiled=True),
    )
    remote_top = back_top[holder_dev, holder_slot]
    remote_mass = back_mass[holder_dev, holder_slot]
    remote_accum = back_accum[holder_dev, holder_slot]
    own_query = query_rot[:dec_count].astype(jnp.float32)
    own_key = my_keys[:dec_count].astype(jnp.float32)
    own_value = my_values[:dec_count].astype(jnp.float32)
    own_score = (
        jnp.einsum("shd,sd->sh", own_query, own_key, precision=lax.Precision.HIGHEST) * score_scale
    )
    final_top = jnp.maximum(remote_top, own_score)
    remote_factor = jnp.exp(remote_top - final_top)
    own_factor = jnp.exp(own_score - final_top)
    numerator = (
        remote_accum * remote_factor[..., None] + own_factor[..., None] * own_value[:, None, :]
    )
    denominator = remote_mass * remote_factor + own_factor
    decode_out = (
        (numerator / denominator[..., None])
        .reshape(dec_count, heads_local * HD)
        .astype(jnp.bfloat16)
    )
    attention_out = jnp.concatenate([decode_out, prompt_out], axis=0)
    return (hidden_out, new_cache, attention_out)


def solution(mesh):
    return jax.shard_map(
        shards,
        mesh=mesh,
        in_specs=(
            P("row", "col"),
            P("row", "col"),
            P("col", None),
            P(),
            P(),
            P("row", None),
            P("row", None),
            P(("row", "col"), None, None),
            P(("row", "col"), None, None),
            P(("row", "col"), None, None),
            P(None, "col"),
            P(None, "col"),
            P("row", None),
            P("row"),
            P("row"),
            P("row", "col", None),
            P("row", "col", None),
        ),
        out_specs=(P("row", "col"), P("row", "col"), P("row", "col")),
        check_vma=False,
    )
```

profile of v0, /device:TPU:1, one launch (start us, length us, event | category | flops | bytes accessed | tf_op | source)
XLA Modules:
  0.0 782.1 jit_solution(6182529554980959249)
XLA Ops:
  7.2 4.1 fusion.103
  11.4 102.1 %reduce-scatter.3.cloned.1.call-done = f32[512,128]{1,0:T(8,128)} async-done(((f32[512,2048]{1,0:T(8,128)}), f32[512,128]{1,0:T(8,128)}) %reduce-scatter.3.cloned.1.call-update) | async-done | bytes 262160 | tf_op jit(solution)/shard_map/reduce_scatter | solution.py:89
  113.5 1.6 add_convert_fusion.1
  115.3 1.2 reduce-window.6
  117.4 30.4 %scatter_custom_fusion.3 = s32[1024]{0:T(1024)S(1)} fusion(s32[8192]{0:T(1024)S(1)} %reshape.353, s32[8192]{0:T(1024)S(1)} %reshape.355, s32[]{:T(128)} %constant.121.clone.1), kind=kCustom, calls=%fused_computation.150 | custom fusion | bytes 4100
  148.0 42.8 %all-gather.5.cloned.1.call-done = bf16[512,2048]{1,0:T(8,128)(2,1)} async-done(((bf16[512,128]{1,0:T(8,128)(2,1)}), bf16[512,2048]{1,0:T(8,128)(2,1)}) %all-gather.5.cloned.1.call-update) | async-done | bytes 2097168 | tf_op jit(solution)/shard_map/all_gather | solution.py:50
  190.8 2.2 fusion.4
  193.6 1.5 concatenate.52
  195.0 10.7 %gather_fusion = bf16[1024,2048]{1,0:T(8,128)(2,1)} fusion(bf16[513,2048]{1,0:T(8,128)(2,1)} %concatenate.52, s32[1024]{0:T(1024)S(1)} %broadcast_clamp_fusion), kind=kCustom, calls=%fused_computation | custom fusion | bytes 8392704 | tf_op jit(solution)/shard_map/gather | solution.py:118
  205.7 68.1 %all_to_all.39 = bf16[16,64,2048]{2,1,0:T(8,128)(2,1)S(1)} all-to-all(bf16[16,64,2048]{2,1,0:T(8,128)(2,1)} %bitcast.177), channel_id=1, replica_groups=mesh['row'=16,'col'=16] {'row'}, dimensions={0} | all-to-all | bytes 8388608 | tf_op jit(solution)/shard_map/all_to_all | solution.py:122
  273.9 2.0 copy-done.3
  275.9 3.6 fusion.16
  279.4 7.8 convolution_convert_fusion
  287.2 5.5 all-to-all-start.1
  293.2 30.6 %scatter_custom_fusion.4 = f32[1024]{0:T(1024)S(1)} fusion(s32[8192]{0:T(1024)S(1)} %reshape.353, f32[8192]{0:T(1024)S(1)} %reshape.361, f32[]{:T(128)} %constant.120.clone.1), kind=kCustom, calls=%fused_computation.148 | custom fusion | bytes 4100
  323.9 24.7 %all-to-all-done.1 = bf16[16,64,2048]{2,1,0:T(8,128)(2,1)} async-done(((bf16[16,64,2048]{2,1,0:T(8,128)(2,1)}), bf16[16,64,2048]{2,1,0:T(8,128)(2,1)}, u32[]{:S(2)}, u32[]{:S(2)}) %all-to-all-start.1) | async-done | bytes 4194336 | tf_op jit(solution)/shard_map/all_to_all | solution.py:128
  348.5 6.0 convert_multiply_fusion
  354.5 16.9 %scatter_custom_fusion = f32[512,2048]{1,0:T(8,128)} fusion(s32[1024]{0:T(1024)S(1)} %bitcast.191, f32[1024,2048]{1,0:T(8,128)} %bitcast.178, f32[]{:T(128)} %constant.120.clone.1), kind=kCustom, calls=%fused_computation.30 | custom fusion | flops 2097152 | bytes 4194816 | tf_op jit(solution)/shard_map/scatter-add | solution.py:135
  371.5 98.3 %reduce-scatter.5.cloned.1.call-done = f32[512,128]{1,0:T(8,128)} async-done(((f32[512,2048]{1,0:T(8,128)}), f32[512,128]{1,0:T(8,128)}) %reduce-scatter.5.cloned.1.call-update) | async-done | bytes 262160 | tf_op jit(solution)/shard_map/reduce_scatter | solution.py:137
  469.8 1.6 add_convert_fusion
  473.1 9.1 %all-to-all-start.2 = ((s32[16,1,8]{2,1,0:T(1,128)}), s32[16,1,8]{2,1,0:T(1,128)S(1)}, u32[]{:S(2)}, u32[]{:S(2)}) async-start(s32[16,1,8]{2,1,0:T(1,128)} %copy.82), calls=%async_computation.4 | async-start | bytes 16384 | tf_op jit(solution)/shard_map/all_to_all | solution.py:198
  482.7 1.0 multiply_cosine_fusion
  483.9 63.3 %all-gather.7.cloned.1.call-done = bf16[512,2048]{1,0:T(8,128)(2,1)} async-done(((bf16[512,128]{1,0:T(8,128)(2,1)}), bf16[512,2048]{1,0:T(8,128)(2,1)}) %all-gather.7.cloned.1.call-update) | async-done | bytes 2097168 | tf_op jit(solution)/shard_map/all_gather | solution.py:50
  547.2 2.2 fusion.7
  549.5 1.5 convolution_convert_fusion.3
  551.0 2.5 convolution_convert_fusion.1
  554.2 24.0 %all_gather.24 = bf16[8,4096]{1,0:T(8,128)(2,1)S(1)} all-gather(bf16[8,256]{1,0:T(8,128)(2,1)S(1)} %get-tuple-element.84), channel_id=1, replica_groups=mesh['row'=16,'col'=16] {'col'}, dimensions={1}, use_global_device_ids=true | all-gather | bytes 69632 | tf_op jit(solution)/shard_map/all_gather | solution.py:154
  578.1 1.1 broadcast_in_dim.96
  579.2 3.3 scatter_fusion.1
  582.6 25.2 %all-to-all-start.3 = ((bf16[16,8,4096]{2,1,0:T(8,128)(2,1)}), bf16[16,8,4096]{2,1,0:T(8,128)(2,1)S(1)}, u32[]{:S(2)}, u32[]{:S(2)}) async-start(bf16[16,8,4096]{2,1,0:T(8,128)(2,1)} %scatter_fusion.1), calls=%async_computation.5 | async-start | bytes 2097152 | tf_op jit(solution)/shard_map/all_to_all | solution.py:197
  607.9 18.2 %all-to-all-done.3 = bf16[16,8,4096]{2,1,0:T(8,128)(2,1)S(1)} async-done(((bf16[16,8,4096]{2,1,0:T(8,128)(2,1)}), bf16[16,8,4096]{2,1,0:T(8,128)(2,1)S(1)}, u32[]{:S(2)}, u32[]{:S(2)}) %all-to-all-start.3) | async-done | bytes 1048608 | tf_op jit(solution)/shard_map/all_to_all | solution.py:197
  626.7 1.2 convolution_bitcast_fusion
  629.3 23.3 %all_gather.26 = f32[16,8,32]{2,1,0:T(8,128)S(1)} all-gather(f32[1,8,32]{2,1,0:T(8,128)S(1)} %all_gather_reshape.10), channel_id=1, replica_groups=mesh['row'=16,'col'=16] {'col'}, dimensions={0}, use_global_device_ids=true | all-gather | bytes 17408 | tf_op jit(solution)/shard_map/all_gather | solution.py:18
  652.6 27.1 %all_gather.25 = f32[16,8,32]{2,1,0:T(8,128)S(1)} all-gather(f32[1,8,32]{2,1,0:T(8,128)S(1)} %all_gather_reshape.9), channel_id=1, replica_groups=mesh['row'=16,'col'=16] {'col'}, dimensions={0}, use_global_device_ids=true | all-gather | bytes 17408 | tf_op jit(solution)/shard_map/all_gather | solution.py:18
  679.8 1.3 fusion.97
  681.4 1.0 copy.103
  682.5 1.4 fusion.96
  684.0 2.5 fusion.99
  686.5 3.1 fusion.20
  689.7 1.1 copy.94
  693.9 9.8 %all-gather.11.cloned.1.call-done = f32[16,8,32,128]{3,2,1,0:T(8,128)} async-done(((f32[1,8,32,128]{3,2,1,0:T(8,128)}), f32[16,8,32,128]{3,2,1,0:T(8,128)}) %all-gather.11.cloned.1.call-update) | async-done | bytes 2097168 | tf_op jit(solution)/shard_map/all_gather | solution.py:18
  703.8 3.0 slice.119
  707.7 16.8 %while.14 = (s32[]{:T(128)}, f32[8,32]{1,0:T(8,128)S(1)}, f32[8,32]{1,0:T(8,128)S(1)}, f32[8,32,128]{2,1,0:T(8,128)S(1)}, f32[15,8,32]{2,1,0:T(8,128)S(1)}, /*in...) while((s32[]{:T(128)}, f32[8,32]{1,0:T(8,128)S(1)}, f32[8,32]{1,0:T(8,128)S(1)}, ...), condition=%wide.region_20.21_spmd, body=%wide.region_19.20_spmd.sunk | while | flops 99842 | bytes 403549 | solution.py:21
  707.8 1.2 fusion.116
  709.0 1.1 fusion.116
  710.1 1.1 fusion.116
  711.2 1.1 fusion.116
  712.3 1.1 fusion.116
  713.4 1.1 fusion.116
  714.6 1.1 fusion.116
  715.7 1.1 fusion.116
  716.8 1.1 fusion.116
  717.9 1.1 fusion.116
  719.0 1.1 fusion.116
  720.1 1.1 fusion.116
  721.2 1.1 fusion.116
  722.4 1.1 fusion.116
  723.5 1.1 fusion.116
  725.3 17.1 %all-to-all-start.5 = ((f32[16,8,2]{1,2,0:T(2,128)}), f32[16,8,2]{1,2,0:T(2,128)S(1)}, u32[]{:S(2)}, u32[]{:S(2)}) async-start(f32[16,8,2]{1,2,0:T(2,128)} %broadcast_in_dim.100), calls=%async_computation.7 | async-start | bytes 32768 | tf_op jit(solution)/shard_map/all_to_all | solution.py:228
  742.6 7.1 all-to-all-done.5
  750.3 3.7 all-to-all-start.6
  754.8 6.6 all-to-all-done.6
  762.1 3.7 all-to-all-start.4
  766.5 6.9 all-to-all-done.4
  (169 shorter events, 17.6 us)
Async XLA Ops:
  7.2 272.2 %copy-start = (bf16[1,384,2048]{2,1,0:T(8,128)(2,1)S(1)}, bf16[1,384,2048]{2,1,0:T(8,128)(2,1)}, u32[]{:S(2)}) copy-start(bf16[1,384,2048]{2,1,0:T(8,128)(2,1)} %param.28) | copy-start | bytes 4718596
  7.2 106.3 %reduce-scatter.3.cloned.1.call-start = ((), (), s32[]{:S(2)}) async-start(), calls=%async_computation.9 | async-start | bytes 4456448 | tf_op jit(solution)/shard_map/reduce_scatter | solution.py:89
  11.3 102.2 %copy-start.11 = (bf16[512,128]{1,0:T(8,128)(2,1)S(1)}, bf16[512,128]{1,0:T(8,128)(2,1)}, u32[]{:S(2)}) copy-start(bf16[512,128]{1,0:T(8,128)(2,1)} %param.20) | copy-start | bytes 393220
  11.3 103.8 %copy-start.12 = (s32[512,8]{0,1:T(8,128)S(1)}, s32[512,8]{0,1:T(8,128)}, u32[]{:S(2)}) copy-start(s32[512,8]{0,1:T(8,128)} %param.24) | copy-start | bytes 49156
  11.3 105.5 %copy-start.19 = (s32[2]{0:T(128)S(1)}, s32[2]{0:T(128)}, u32[]{:S(2)}) copy-start(s32[2]{0:T(128)} %constant.155) | copy-start | bytes 28
  11.3 105.6 %copy-start.18 = (s32[2]{0:T(128)S(1)}, s32[2]{0:T(128)}, u32[]{:S(2)}) copy-start(s32[2]{0:T(128)} %constant.158) | copy-start | bytes 28
  11.3 136.7 %copy-start.15 = (bf16[2048]{0:T(1024)(128)(2,1)S(1)}, bf16[2048]{0:T(1024)(128)(2,1)}, u32[]{:S(2)}) copy-start(bf16[2048]{0:T(1024)(128)(2,1)} %param.22) | copy-start | bytes 12292
  11.3 179.4 %all-gather.5.cloned.1.call-start = ((), (), s32[]{:S(2)}) async-start(), calls=%async_computation.10 | async-start | bytes 2228224 | tf_op jit(solution)/shard_map/all_gather | solution.py:50
  190.8 2.2 copy-start.2
  205.7 70.1 %copy-start.20 = (bf16[1,2048,384]{2,1,0:T(8,128)(2,1)S(1)}, bf16[1,2048,384]{2,1,0:T(8,128)(2,1)}, u32[]{:S(2)}) copy-start(bf16[1,2048,384]{2,1,0:T(8,128)(2,1)} %param.26) | copy-start | bytes 4718596
  273.9 2.0 copy-start.3
  275.8 3.6 copy-start.21
  287.2 5.6 copy-start.13
  287.2 61.3 %all-to-all-start.1 = ((bf16[16,64,2048]{2,1,0:T(8,128)(2,1)}), bf16[16,64,2048]{2,1,0:T(8,128)(2,1)}, u32[]{:S(2)}, u32[]{:S(2)}) async-start(bf16[16,64,2048]{2,1,0:T(8,128)(2,1)} %bitcast.179), calls=%async_computation.2 | async-start | bytes 8388608 | tf_op jit(solution)/shard_map/all_to_all | solution.py:128
  292.7 177.1 %reduce-scatter.5.cloned.1.call-start = ((), (), s32[]{:S(2)}) async-start(), calls=%async_computation.11 | async-start | bytes 4456448 | tf_op jit(solution)/shard_map/reduce_scatter | solution.py:137
  371.4 98.4 %copy-start.7 = (bf16[512,128]{1,0:T(8,128)(2,1)S(1)}, bf16[512,128]{1,0:T(8,128)(2,1)}, u32[]{:S(2)}) copy-start(bf16[512,128]{1,0:T(8,128)(2,1)} %add_convert_fusion.1) | copy-start | bytes 393220
  371.4 100.1 %copy-start.25 = (s32[8]{0:T(128)S(1)}, s32[8]{0:T(128)}, u32[]{:S(2)}) copy-start(s32[8]{0:T(128)} %param.33) | copy-start | bytes 100
  371.4 100.1 %copy-start.17 = (s32[8]{0:T(128)S(1)}, s32[8]{0:T(128)}, u32[]{:S(2)}) copy-start(s32[8]{0:T(128)} %param.32) | copy-start | bytes 100
  371.4 111.0 %copy-start.16 = (bf16[2048]{0:T(1024)(128)(2,1)S(1)}, bf16[2048]{0:T(1024)(128)(2,1)}, u32[]{:S(2)}) copy-start(bf16[2048]{0:T(1024)(128)(2,1)} %param.23) | copy-start | bytes 12292
  371.4 111.0 %copy-start.14 = (s32[1,504]{1,0:T(1,128)S(1)}, s32[1,504]{1,0:T(1,128)}, u32[]{:S(2)}) copy-start(s32[1,504]{1,0:T(1,128)} %param.31) | copy-start | bytes 6052
  371.5 175.8 %all-gather.7.cloned.1.call-start = ((), (), s32[]{:S(2)}) async-start(), calls=%async_computation.12 | async-start | bytes 2228224 | tf_op jit(solution)/shard_map/all_gather | solution.py:50
  472.4 77.1 %copy-start.24 = (bf16[2048,64]{0,1:T(8,128)(2,1)S(1)}, bf16[2048,64]{0,1:T(8,128)(2,1)}, u32[]{:S(2)}) copy-start(bf16[2048,64]{0,1:T(8,128)(2,1)} %param.30) | copy-start | bytes 786436
  473.1 109.5 %all-to-all-start.2 = ((s32[16,1,8]{2,1,0:T(1,128)}), s32[16,1,8]{2,1,0:T(1,128)S(1)}, u32[]{:S(2)}, u32[]{:S(2)}) async-start(s32[16,1,8]{2,1,0:T(1,128)} %copy.82), calls=%async_computation.4 | async-start | bytes 16384 | tf_op jit(solution)/shard_map/all_to_all | solution.py:198
  482.2 197.6 %all-gather.9.cloned.1.call-start = ((), (), s32[]{:S(2)}) async-start(), calls=%async_computation.13 | async-start | bytes 1114112 | tf_op jit(solution)/shard_map/all_gather | solution.py:153
  547.2 2.3 copy-start.6
  549.5 1.6 copy-start.22
  579.2 47.0 %copy-start.8 = (bf16[8,64,512]{2,1,0:T(8,128)(2,1)S(1)}, bf16[8,64,512]{2,1,0:T(8,128)(2,1)}, u32[]{:S(2)}) copy-start(bf16[8,64,512]{2,1,0:T(8,128)(2,1)} %param.34) | copy-start | bytes 1572868
  582.6 44.1 %copy-start.23 = (bf16[8,64,512]{2,1,0:T(8,128)(2,1)S(1)}, bf16[8,64,512]{2,1,0:T(8,128)(2,1)}, u32[]{:S(2)}) copy-start(bf16[8,64,512]{2,1,0:T(8,128)(2,1)} %param.35) | copy-start | bytes 1572868
  582.6 43.5 %all-to-all-start.3 = ((bf16[16,8,4096]{2,1,0:T(8,128)(2,1)}), bf16[16,8,4096]{2,1,0:T(8,128)(2,1)S(1)}, u32[]{:S(2)}, u32[]{:S(2)}) async-start(bf16[16,8,4096]{2,1,0:T(8,128)(2,1)} %scatter_fusion.1), calls=%async_computation.5 | async-start | bytes 2097152 | tf_op jit(solution)/shard_map/all_to_all | solution.py:197
  607.8 96.0 %all-gather.11.cloned.1.call-start = ((), (), s32[]{:S(2)}) async-start(), calls=%async_computation.14 | async-start | bytes 2228224 | tf_op jit(solution)/shard_map/all_gather | solution.py:18
  652.6 29.7 %copy-start.9 = (f32[16,8,32]{2,1,0:T(8,128)}, f32[16,8,32]{2,1,0:T(8,128)S(1)}, u32[]{:S(2)}) copy-start(f32[16,8,32]{2,1,0:T(8,128)S(1)} %all_gather.26) | copy-start | bytes 49156
  679.8 2.6 copy-start.10
  686.5 4.3 copy-start.4
  690.8 1.1 copy-start.5
  693.9 13.8 %slice-start = ((f32[16,8,32]{2,1,0:T(8,128)}), f32[15,8,32]{2,1,0:T(8,128)S(1)}, s32[]{:S(2)}) async-start(f32[16,8,32]{2,1,0:T(8,128)} %copy-done.9), calls=%async_computation.15 | async-start | bytes 122880 | tf_op jit(solution)/shard_map/slice | solution.py:20
  693.9 13.8 %slice-start.1 = ((f32[16,8,32]{2,1,0:T(8,128)}), f32[15,8,32]{2,1,0:T(8,128)S(1)}, s32[]{:S(2)}) async-start(f32[16,8,32]{2,1,0:T(8,128)} %copy-done.10), calls=%async_computation.16 | async-start | bytes 122880 | tf_op jit(solution)/shard_map/slice | solution.py:20
  707.7 67.5 %copy-start.1 = (bf16[1,384,2048]{2,1,0:T(8,128)(2,1)S(1)}, bf16[1,384,2048]{2,1,0:T(8,128)(2,1)}, u32[]{:S(2)}) copy-start(bf16[1,384,2048]{2,1,0:T(8,128)(2,1)} %param.28) | copy-start | bytes 4718596
  725.3 24.4 %all-to-all-start.5 = ((f32[16,8,2]{1,2,0:T(2,128)}), f32[16,8,2]{1,2,0:T(2,128)S(1)}, u32[]{:S(2)}, u32[]{:S(2)}) async-start(f32[16,8,2]{1,2,0:T(2,128)} %broadcast_in_dim.100), calls=%async_computation.7 | async-start | bytes 32768 | tf_op jit(solution)/shard_map/all_to_all | solution.py:228
  750.3 11.0 %all-to-all-start.6 = ((f32[16,8,2]{1,2,0:T(2,128)}), f32[16,8,2]{1,2,0:T(2,128)S(1)}, u32[]{:S(2)}, u32[]{:S(2)}) async-start(f32[16,8,2]{1,2,0:T(2,128)} %broadcast_in_dim.101), calls=%async_computation.8 | async-start | bytes 32768 | tf_op jit(solution)/shard_map/all_to_all | solution.py:229
  762.1 11.4 %all-to-all-start.4 = ((f32[16,8,2,128]{3,2,1,0:T(2,128)}), f32[16,8,2,128]{3,2,1,0:T(2,128)S(1)}, u32[]{:S(2)}, u32[]{:S(2)}) async-start(f32[16,8,2,128]{3,2,1,0:T(2,128)} %broadcast_in_dim.99), calls=%async_computation.6 | async-start | bytes 262144 | tf_op jit(solution)/shard_map/all_to_all | solution.py:230
Sparse Core Ops, SparseCore 0:
  11.5 101.9 reduce-scatter.2
  115.7 74.9 all-gather.4
  371.6 98.2 reduce-scatter.4
  472.0 75.2 all-gather.6
  551.1 76.7 all-gather.8
  629.5 74.1 all-gather.10
where the time goes:
time: 783 us; the launch traced here: 782 us
  waiting for transfers between devices  380 us (49%)
  blocking collectives  143 us (18%)
  local copies, waits for them, and re-layouts  97.3 us (12%)
  starting transfers between devices  64.7 us (8%)
  other arithmetic  55.6 us (7%)
  matrix products  26.9 us (3%)
  between operations  14.7 us (2%)
    all_gather x2, waiting for transfers between devices, spread_norm(): gathered = lax.all_gather(hidden, 'col', axis=1, tiled=True)  106 us
    reduce_scatter x1, waiting for transfers between devices, shards(): summed = lax.psum_scatter(projected, 'col', scatter_dimension=1, tiled=True)  102 us
    reduce_scatter x1, waiting for transfers between devices, shards(): lax.psum_scatter(partial_moe, 'col', scatter_dimension=1, tiled=True)  98.3 us
    all_to_all x1, blocking collectives, shards(): lax.all_to_all(outgoing, 'row', split_axis=0, concat_axis=0, tiled=True)  68.1 us
    unnamed x59, local copies, waits for them, and re-layouts  66.1 us
    all_gather x2, blocking collectives, merged_2(): pieces = jax.tree.map(lambda part: lax.all_gather(part, axis), value)  50.5 us
    all_to_all x1, starting transfers between devices, shards(): lax.all_to_all(outbox, 'row', split_axis=0, concat_axis=0, tiled=True)  25.2 us
    all_to_all x1, waiting for transfers between devices, shards(): lax.all_to_all(result.reshape(arrived.shape), 'row', split_axis=0, concat...  24.7 us
  transfers between devices with their start and end apart: 12, of which 10 were waited for; matrix products, arithmetic and copies ran while one was open for 12% of the time, Pallas kernels for 0%

commit v1 on v0

--- a/solution.py
+++ b/solution.py
@@ -1,17 +1,408 @@
+import functools
+
 import jax
 import jax.numpy as jnp
 from jax import lax
+from jax.experimental import pallas as pl
+from jax.experimental.pallas import tpu as pltpu
 from jax.sharding import PartitionSpec as P
 
 TOP = 8
 QH = 32
 KVH = 4
 HD = 128
-
-
 EPSILON = 1e-06
 ROPE_THETA = 1000000.0
 NEGATIVE = -1e30
+MESH = pl.DeviceIdType.MESH
+
+D = 2048
+HALF_D = 1024
+LEFT = pl.ds(0, HALF_D)
+RIGHT = pl.ds(HALF_D, HALF_D)
+ROWS = 512
+BLOCK = 32
+CAP = 64
+RING_SEMS = 23
+TILE = 512
+
+
+def remote(src, dst, send, recv, index, device):
+    return pltpu.make_async_remote_copy(
+        src_ref=src,
+        dst_ref=dst,
+        send_sem=send.at[index],
+        recv_sem=recv.at[index],
+        device_id=device,
+        device_id_type=MESH,
+    )
+
+
+def around():
+    row = lax.axis_index("row")
+    col = lax.axis_index("col")
+    z = col // 2
+    y = lax.rem(col, 2)
+    after = (row, lax.rem(z + 1, 8) * 2 + y)
+    before = (row, lax.rem(z + 7, 8) * 2 + y)
+    beside = (row, z * 2 + 1 - y)
+    return z, y, after, before, beside
+
+
+def reduce_blocks(place, blocks, y_left, up_left, down_left, up_right, down_right, y_right, send, recv, base):
+    z, y, after, before, beside = place
+    other = 1 - y
+    started = []
+
+    def go(src, dst, index, device):
+        copy = remote(src, dst, send, recv, base + index, device)
+        copy.start()
+        started.append(copy)
+        return copy
+
+    def at(offset):
+        return lax.rem(z + offset + 8, 8)
+
+    crossing = {}
+    for index, offset in enumerate((4, -3, 3, -2, 2, -1, 1, 0)):
+        t = at(offset)
+        crossing[offset] = go(blocks.at[other, t, :, LEFT], y_left.at[t], index, beside)
+    up_l, down_l, up_r, down_r = [], [], [], []
+    for step in range(4):
+        if step < 3:
+            t = at(3 - step)
+            if step:
+                up_r[-1].wait_recv()
+                blocks[:, t, :, RIGHT] = (
+                    blocks[:, t, :, RIGHT].astype(jnp.float32) + up_right[step - 1].astype(jnp.float32)
+                ).astype(jnp.bfloat16)
+            up_r.append(go(blocks.at[:, t, :, RIGHT], up_right.at[step], 8 + step, after))
+        t = at(step - 4)
+        if step:
+            down_r[-1].wait_recv()
+            blocks[:, t, :, RIGHT] = (
+                blocks[:, t, :, RIGHT].astype(jnp.float32) + down_right[step - 1].astype(jnp.float32)
+            ).astype(jnp.bfloat16)
+        down_r.append(go(blocks.at[:, t, :, RIGHT], down_right.at[step], 11 + step, before))
+        t = at(4 - step)
+        crossing[4 - step].wait_recv()
+        value = blocks[y, t, :, LEFT].astype(jnp.float32) + y_left[t].astype(jnp.float32)
+        if step:
+            up_l[-1].wait_recv()
+            value = value + up_left[step - 1].astype(jnp.float32)
+        blocks[y, t, :, LEFT] = value.astype(jnp.bfloat16)
+        up_l.append(go(blocks.at[y, t, :, LEFT], up_left.at[step], 15 + step, after))
+        if step < 3:
+            t = at(step - 3)
+            crossing[step - 3].wait_recv()
+            value = blocks[y, t, :, LEFT].astype(jnp.float32) + y_left[t].astype(jnp.float32)
+            if step:
+                down_l[-1].wait_recv()
+                value = value + down_left[step - 1].astype(jnp.float32)
+            blocks[y, t, :, LEFT] = value.astype(jnp.bfloat16)
+            down_l.append(go(blocks.at[y, t, :, LEFT], down_left.at[step], 19 + step, before))
+    up_r[-1].wait_recv()
+    down_r[-1].wait_recv()
+    blocks[other, z, :, RIGHT] = (
+        blocks[other, z, :, RIGHT].astype(jnp.float32)
+        + up_right[2, other].astype(jnp.float32)
+        + down_right[3, other].astype(jnp.float32)
+    ).astype(jnp.bfloat16)
+    last = go(blocks.at[other, z, :, RIGHT], y_right, 22, beside)
+    right = (
+        blocks[y, z, :, RIGHT].astype(jnp.float32)
+        + up_right[2, y].astype(jnp.float32)
+        + down_right[3, y].astype(jnp.float32)
+    )
+    crossing[0].wait_recv()
+    up_l[-1].wait_recv()
+    down_l[-1].wait_recv()
+    left = (
+        blocks[y, z, :, LEFT].astype(jnp.float32)
+        + y_left[z].astype(jnp.float32)
+        + up_left[3].astype(jnp.float32)
+        + down_left[2].astype(jnp.float32)
+    )
+    last.wait_recv()
+    right = right + y_right[...].astype(jnp.float32)
+    return left, right, started
+
+
+def gather_blocks(place, full, send, recv, base):
+    z, y, after, before, beside = place
+    started = []
+
+    def go(view, index, device):
+        copy = remote(view, view, send, recv, base + index, device)
+        copy.start()
+        started.append(copy)
+        return copy
+
+    def at(offset):
+        return lax.rem(z + offset + 8, 8)
+
+    first = go(full.at[z, y, :, RIGHT], 0, beside)
+    crossing = []
+    up_l, down_l, up_r, down_r = [], [], [], []
+
+    def cross(t):
+        crossing.append(go(full.at[t, y, :, LEFT], 1 + len(crossing), beside))
+
+    for step in range(4):
+        if step:
+            up_l[-1].wait_recv()
+        up_l.append(go(full.at[at(-step), y, :, LEFT], 9 + step, after))
+        if step < 3:
+            if step:
+                down_l[-1].wait_recv()
+            down_l.append(go(full.at[at(step), y, :, LEFT], 13 + step, before))
+        if step == 0:
+            first.wait_recv()
+        if step < 3:
+            if step:
+                up_r[-1].wait_recv()
+            up_r.append(go(full.at[at(-step), :, :, RIGHT], 16 + step, after))
+        if step:
+            down_r[-1].wait_recv()
+        down_r.append(go(full.at[at(step), :, :, RIGHT], 19 + step, before))
+        cross(at(-step))
+        if 0 < step < 3:
+            cross(at(step))
+    down_l[-1].wait_recv()
+    cross(at(3))
+    up_l[-1].wait_recv()
+    cross(at(-4))
+    up_r[-1].wait_recv()
+    down_r[-1].wait_recv()
+    for copy in crossing:
+        copy.wait_recv()
+    return started
+
+
+def ring_scratch():
+    return [
+        pltpu.VMEM((2, 8, BLOCK, D), jnp.bfloat16),
+        pltpu.VMEM((8, BLOCK, HALF_D), jnp.bfloat16),
+        pltpu.VMEM((4, BLOCK, HALF_D), jnp.bfloat16),
+        pltpu.VMEM((3, BLOCK, HALF_D), jnp.bfloat16),
+        pltpu.VMEM((3, 2, BLOCK, HALF_D), jnp.bfloat16),
+        pltpu.VMEM((4, 2, BLOCK, HALF_D), jnp.bfloat16),
+        pltpu.VMEM((BLOCK, HALF_D), jnp.bfloat16),
+    ]
+
+
+def greet(devices):
+    barrier = pltpu.get_barrier_semaphore()
+    for device in devices:
+        pl.semaphore_signal(barrier, inc=1, device_id=device, device_id_type=MESH)
+    return barrier
+
+
+def by_block(value):
+    return value.reshape(8, 2, BLOCK, value.shape[-1])
+
+
+def out_kernel(context, w_out, residual, gain, normed, mid, blocks, *rest):
+    buffers, (send, recv) = rest[:6], rest[6:]
+    place = around()
+    z, y, after, before, beside = place
+    barrier = greet((after, before, beside))
+    for tile in range(0, D, TILE):
+        columns = pl.ds(tile, TILE)
+        value = by_block(
+            jnp.dot(context[...], w_out[:, columns], preferred_element_type=jnp.float32).astype(jnp.bfloat16)
+        )
+        blocks[0, :, :, columns] = value[:, 0]
+        blocks[1, :, :, columns] = value[:, 1]
+    own = pl.ds(pl.multiple_of((z * 2 + y) * 128, 128), 128)
+    value = jnp.dot(context[...], w_out[:, own], preferred_element_type=jnp.float32)
+    value = by_block((value + residual[...].astype(jnp.float32)).astype(jnp.bfloat16))
+    blocks[0, :, :, own] = value[:, 0]
+    blocks[1, :, :, own] = value[:, 1]
+    pl.semaphore_wait(barrier, 3)
+    left, right, started = reduce_blocks(place, blocks, *buffers, send, recv, 0)
+    left = left.astype(jnp.bfloat16)
+    right = right.astype(jnp.bfloat16)
+    mid[:, :HALF_D] = left
+    mid[:, HALF_D:] = right
+    left = left.astype(jnp.float32)
+    right = right.astype(jnp.float32)
+    mean = (
+        jnp.sum(left * left, axis=-1, keepdims=True) + jnp.sum(right * right, axis=-1, keepdims=True)
+    ) * (1.0 / D)
+    inverse = lax.rsqrt(mean + EPSILON)
+    gains = gain[...].astype(jnp.float32)
+    normed[z, y, :, LEFT] = (left * inverse * gains[:, :HALF_D]).astype(jnp.bfloat16)
+    normed[z, y, :, RIGHT] = (right * inverse * gains[:, HALF_D:]).astype(jnp.bfloat16)
+    started = started + gather_blocks(place, normed, send, recv, RING_SEMS)
+    for copy in started:
+        copy.wait_send()
+
+
+def out_project(context, w_out, residual, gain):
+    vmem = pl.BlockSpec(memory_space=pltpu.VMEM)
+    return pl.pallas_call(
+        out_kernel,
+        out_shape=(
+            jax.ShapeDtypeStruct((8, 2, BLOCK, D), jnp.bfloat16),
+            jax.ShapeDtypeStruct((BLOCK, D), jnp.bfloat16),
+        ),
+        in_specs=[vmem] * 4,
+        out_specs=(vmem, vmem),
+        scratch_shapes=ring_scratch()
+        + [pltpu.SemaphoreType.DMA((2 * RING_SEMS,)), pltpu.SemaphoreType.DMA((2 * RING_SEMS,))],
+        compiler_params=pltpu.CompilerParams(
+            collective_id=0, has_side_effects=True, vmem_limit_bytes=40 << 20
+        ),
+        name="out_project",
+    )(context, w_out, residual, gain.reshape(1, D))
+
+
+GROUPS = (8, 12, 4, 0)
+
+
+def expert_kernel(
+    normed, routes, scores, w_gate, w_up, w_down, mid, full, share,
+    blocks, y_left, up_left, down_left, up_right, down_right, y_right,
+    going, coming, back, total, weights, send, recv,
+):
+    row = lax.axis_index("row")
+    place = around()
+    z, y, after, before, beside = place
+    yh, x, core = row // 8, lax.rem(row // 2, 4), lax.rem(row, 2)
+
+    def partner(o, sign):
+        a, b, d = o // 8, (o // 2) % 4, o % 2
+        there = lax.rem(yh + a, 2) * 8 + lax.rem(x + sign * b + 4, 4) * 2 + lax.rem(core + d, 2)
+        return (there, z * 2 + lax.rem(y + a, 2))
+
+    partners = [partner(o, 1) for o in range(1, 16)]
+    barrier = greet([after, before, beside] + partners)
+    offsets = lax.broadcasted_iota(jnp.int32, (16, 1), 0)
+    a, b, d = offsets // 8, lax.rem(offsets // 2, 4), lax.rem(offsets, 2)
+    expert = (
+        lax.rem(yh + a, 2) * 8 + lax.rem(x + b, 4) * 2 + lax.rem(core + d, 2)
+    ) * 8 + z
+    score = scores[...]
+    share_of = score / jnp.sum(score, axis=0, keepdims=True)
+    hit = jnp.zeros((16, ROWS), jnp.float32)
+    weight = jnp.zeros((16, ROWS), jnp.float32)
+    for choice in range(TOP):
+        match = routes[choice : choice + 1, :] == expert
+        hit = hit + jnp.where(match, 1.0, 0.0)
+        weight = weight + jnp.where(match, share_of[choice : choice + 1, :], 0.0)
+    earlier = lax.broadcasted_iota(jnp.int32, (ROWS, ROWS), 0) < lax.broadcasted_iota(
+        jnp.int32, (ROWS, ROWS), 1
+    )
+    rank = jnp.dot(
+        hit.astype(jnp.bfloat16),
+        jnp.where(earlier, 1.0, 0.0).astype(jnp.bfloat16),
+        preferred_element_type=jnp.float32,
+    )
+    rank = jnp.where(hit > 0.0, rank, -1.0).astype(jnp.int32)
+    slots = lax.broadcasted_iota(jnp.int32, (CAP, ROWS), 0)
+    pl.semaphore_wait(barrier, 18)
+    started = []
+    arrivals = {}
+    for group in GROUPS:
+        picks = []
+        for o in range(group, group + 4):
+            chosen = slots == rank[o : o + 1, :]
+            picks.append(jnp.where(chosen, 1.0, 0.0).astype(jnp.bfloat16))
+            weights[o * CAP : (o + 1) * CAP, :] = jnp.where(chosen, weight[o : o + 1, :], 0.0).astype(
+                jnp.bfloat16
+            )
+        pick = jnp.concatenate(picks, axis=0)
+        for tile in range(0, D, TILE):
+            columns = pl.ds(tile, TILE)
+            value = jnp.dot(pick, normed[:, columns], preferred_element_type=jnp.float32)
+            value = value.astype(jnp.bfloat16).reshape(4, CAP, TILE)
+            if group:
+                going[group : group + 4, :, columns] = value
+            else:
+                coming[0, :, columns] = value[0]
+                going[1:4, :, columns] = value[1:]
+        for o in range(max(group, 1), group + 4):
+            copy = remote(going.at[o], coming.at[o], send, recv, o, partner(o, 1))
+            copy.start()
+            started.append(copy)
+            arrivals[o] = copy
+    returns = {}
+    for group in GROUPS:
+        for o in range(max(group, 1), group + 4):
+            arrivals[o].wait_recv()
+        rows = coming[group : group + 4].reshape(4 * CAP, D)
+        gate = jnp.dot(rows, w_gate[...], preferred_element_type=jnp.float32)
+        up = jnp.dot(rows, w_up[...], preferred_element_type=jnp.float32)
+        inner = (gate / (1.0 + jnp.exp(-gate)) * up).astype(jnp.bfloat16)
+        for tile in range(0, D, TILE):
+            columns = pl.ds(tile, TILE)
+            value = jnp.dot(inner, w_down[:, columns], preferred_element_type=jnp.float32)
+            coming[group : group + 4, :, columns] = value.astype(jnp.bfloat16).reshape(4, CAP, TILE)
+        for o in range(max(group, 1), group + 4):
+            copy = remote(coming.at[o], back.at[o], send, recv, 16 + o, partner(o, -1))
+            copy.start()
+            started.append(copy)
+            returns[o] = copy
+    back[0] = coming[0]
+    for index, group in enumerate(GROUPS[::-1]):
+        for o in range(max(group, 1), group + 4):
+            returns[o].wait_recv()
+        spread = weights[group * CAP : (group + 4) * CAP, :]
+        for tile in range(0, D, TILE):
+            columns = pl.ds(tile, TILE)
+            value = lax.dot_general(
+                spread,
+                back[group : group + 4, :, columns].reshape(4 * CAP, TILE),
+                (((0,), (0,)), ((), ())),
+                preferred_element_type=jnp.float32,
+            )
+            if index:
+                value = value + total[:, columns]
+            if index < 3:
+                total[:, columns] = value
+            else:
+                value = by_block(value.astype(jnp.bfloat16))
+                blocks[0, :, :, columns] = value[:, 0]
+                blocks[1, :, :, columns] = value[:, 1]
+    left, right, ring = reduce_blocks(
+        place, blocks, y_left, up_left, down_left, up_right, down_right, y_right, send, recv, 32
+    )
+    full[z, y, :, LEFT] = (mid[:, :HALF_D].astype(jnp.float32) + left).astype(jnp.bfloat16)
+    full[z, y, :, RIGHT] = (mid[:, HALF_D:].astype(jnp.float32) + right).astype(jnp.bfloat16)
+    started = started + ring + gather_blocks(place, full, send, recv, 32 + RING_SEMS)
+    own = pl.ds(pl.multiple_of((z * 2 + y) * 128, 128), 128)
+    share[...] = full[:, :, :, own].reshape(ROWS, 128)
+    for copy in started:
+        copy.wait_send()
+
+
+def experts(normed, routes, scores, w_gate, w_up, w_down, mid):
+    vmem = pl.BlockSpec(memory_space=pltpu.VMEM)
+    sems = 32 + 2 * RING_SEMS
+    return pl.pallas_call(
+        expert_kernel,
+        out_shape=(
+            jax.ShapeDtypeStruct((8, 2, BLOCK, D), jnp.bfloat16),
+            jax.ShapeDtypeStruct((ROWS, 128), jnp.bfloat16),
+        ),
+        in_specs=[vmem] * 7,
+        out_specs=(vmem, vmem),
+        scratch_shapes=ring_scratch()
+        + [
+            pltpu.VMEM((16, CAP, D), jnp.bfloat16),
+            pltpu.VMEM((16, CAP, D), jnp.bfloat16),
+            pltpu.VMEM((16, CAP, D), jnp.bfloat16),
+            pltpu.VMEM((ROWS, D), jnp.float32),
+            pltpu.VMEM((16 * CAP, ROWS), jnp.bfloat16),
+            pltpu.SemaphoreType.DMA((sems,)),
+            pltpu.SemaphoreType.DMA((sems,)),
+        ],
+        compiler_params=pltpu.CompilerParams(
+            collective_id=1, has_side_effects=True, vmem_limit_bytes=52 << 20
+        ),
+        name="experts",
+    )(normed, routes, scores, w_gate, w_up, w_down, mid)
 
 
 def merged_2(value, axis, join):
@@ -44,11 +435,6 @@
 def segment_positions(segment_rows):
     earlier = jnp.sum((segment_rows[None, :] < segment_rows[:, None]).astype(jnp.int32), axis=1)
     return jnp.arange(segment_rows.shape[0], dtype=jnp.int32) - earlier
-
-
-def spread_norm(hidden, gain_vector):
-    gathered = lax.all_gather(hidden, "col", axis=1, tiled=True)
-    return (gathered, rms_norm(gathered, gain_vector))
 
 
 def join_partials(first, second):
@@ -83,60 +469,17 @@
     col_count = lax.axis_size("col")
     row_count = lax.axis_size("row")
     tok_rows = attn_context.shape[0]
-    share_width = residual.shape[1]
-    model_width = share_width * col_count
-    projected = jnp.dot(attn_context, w_out, preferred_element_type=jnp.float32)
-    summed = lax.psum_scatter(projected, "col", scatter_dimension=1, tiled=True)
-    hidden_mid = (residual.astype(jnp.float32) + summed).astype(jnp.bfloat16)
-    full_mid, normed = spread_norm(hidden_mid, gain_post)
-    group_width = col_count // 2
-    expert_count = row_count * group_width
-    capacity = 2 * tok_rows * TOP // expert_count
-    route_weight = router_scores / jnp.sum(router_scores, axis=1, keepdims=True)
-    matching = routes % group_width == col_index // 2
-    target = routes // group_width
-    dest_ids = jnp.arange(row_count, dtype=jnp.int32)
-    hitting = matching[:, :, None] & (target[:, :, None] == dest_ids[None, None, :])
-    sent_flag = jnp.sum(hitting.astype(jnp.int32), axis=1)
-    sent_weight = jnp.sum(jnp.where(hitting, route_weight[:, :, None], 0.0), axis=1)
-    place = jnp.cumsum(sent_flag, axis=0) - sent_flag
-    dest_or_drop = jnp.where(sent_flag > 0, dest_ids[None, :], row_count)
-    row_ids = jnp.broadcast_to(
-        jnp.arange(tok_rows, dtype=jnp.int32)[:, None], (tok_rows, row_count)
-    )
-    slot_rows = (
-        jnp.full((row_count, capacity), tok_rows, jnp.int32)
-        .at[dest_or_drop, place]
-        .set(row_ids, mode="drop")
-    )
-    slot_weight = (
-        jnp.zeros((row_count, capacity), jnp.float32)
-        .at[dest_or_drop, place]
-        .set(sent_weight, mode="drop")
-    )
-    padded = jnp.concatenate([normed, jnp.zeros((1, model_width), jnp.bfloat16)], axis=0)
-    outgoing = padded[slot_rows]
-    gate_local = w_gate[0]
-    up_local = w_up[0]
-    down_local = w_down[0]
-    arrived = lax.all_to_all(outgoing, "row", split_axis=0, concat_axis=0, tiled=True)
-    flat_rows = arrived.reshape(-1, arrived.shape[2])
-    gate_part = jnp.dot(flat_rows, gate_local, preferred_element_type=jnp.float32)
-    up_part = jnp.dot(flat_rows, up_local, preferred_element_type=jnp.float32)
-    inner = (jax.nn.silu(gate_part) * up_part).astype(jnp.bfloat16)
-    result = jnp.dot(inner, down_local, preferred_element_type=jnp.float32).astype(jnp.bfloat16)
-    returned = lax.all_to_all(
-        result.reshape(arrived.shape), "row", split_axis=0, concat_axis=0, tiled=True
-    )
-    weighted = slot_weight[:, :, None] * returned.astype(jnp.float32)
-    partial_moe = (
-        jnp.zeros((tok_rows, model_width), jnp.float32)
-        .at[slot_rows.reshape(-1)]
-        .add(weighted.reshape(-1, model_width), mode="drop")
-    )
-    moe_share = lax.psum_scatter(partial_moe, "col", scatter_dimension=1, tiled=True)
-    hidden_out = (hidden_mid.astype(jnp.float32) + moe_share).astype(jnp.bfloat16)
-    _, x_in = spread_norm(hidden_out, gain_input)
+    normed, mid = out_project(attn_context, w_out, residual, gain_post)
+    full, hidden_out = experts(
+        normed.reshape(tok_rows, D),
+        routes.T,
+        router_scores.T,
+        w_gate[0],
+        w_up[0],
+        w_down[0],
+        mid,
+    )
+    x_in = rms_norm(full.reshape(tok_rows, D), gain_input)
     heads_local = QH // col_count
     dec_count = cache_lengths.shape[0]
     score_scale = HD ** (-0.5)

time: 783 us -> 496 us (0.63)
  waiting for transfers between devices: 380 us -> 36.2 us
  Pallas kernels: 0 us -> 232 us
  blocking collectives: 143 us -> 74.3 us
  local copies, waits for them, and re-layouts: 97.3 us -> 32.3 us
  other arithmetic: 55.6 us -> 31.8 us
  matrix products: 26.9 us -> 9.72 us
    pallas_call x0 -> x2, Pallas kernels: none -> 232 us  [the longest x1 185 us: experts(): pl.pallas_call(expert_kernel, out_shape=(jax.ShapeDtypeStruct((8, 2, BLOC...]
    reduce_scatter x2 -> x0, waiting for transfers between devices: 200 us -> none  [the longest x1 102 us: shards(): summed = lax.psum_scatter(projected, 'col', scatter_dimension=1, tiled=True)]
    all_gather x2 -> x0, waiting for transfers between devices: 106 us -> none  [spread_norm(): gathered = lax.all_gather(hidden, 'col', axis=1, tiled=True)]
    all_to_all x1 -> x0, blocking collectives: 68.1 us -> none  [shards(): lax.all_to_all(outgoing, 'row', split_axis=0, concat_axis=0, tiled=True)]
    unnamed x59 -> x36, local copies, waits for them, and re-layouts: 66.1 us -> 10.2 us
    all_to_all x1 -> x0, waiting for transfers between devices: 24.7 us -> none  [shards(): lax.all_to_all(result.reshape(arrived.shape), 'row', split_axis=0, concat...]
    scatter-add x1 -> x0, other arithmetic: 16.9 us -> none  [shards(): partial_moe = jnp.zeros((tok_rows, model_width), jnp.float32).at[slot_row...]
    dot_general x3 -> x0, matrix products: 15.4 us -> none  [the longest x1 7.8 us: shards(): jnp.dot(inner, down_local, preferred_element_type=jnp.float32)]
  transfers between devices with their start and end apart: 12 -> 7, of which waited for: 10 -> 4; matrix products, arithmetic and copies ran while one was open for 12% -> 9% of each run, Pallas kernels for 0% -> 47%
where the time goes in v1:
time: 496 us; the launch traced here: 494 us
  Pallas kernels  232 us (47%)
  blocking collectives  74.3 us (15%)
  starting transfers between devices  62.6 us (13%)
  waiting for transfers between devices  36.2 us (7%)
  local copies, waits for them, and re-layouts  32.3 us (7%)
  other arithmetic  31.8 us (6%)
  between operations  14.3 us (3%)
  matrix products  9.72 us (2%)
    pallas_call x1, Pallas kernels, experts(): pl.pallas_call(expert_kernel, out_shape=(jax.ShapeDtypeStruct((8, 2, BLOC...  185 us
    all_gather x2, blocking collectives, merged_2(): pieces = jax.tree.map(lambda part: lax.all_gather(part, axis), value)  50 us
    pallas_call x1, Pallas kernels, out_project(): pl.pallas_call(out_kernel, out_shape=(jax.ShapeDtypeStruct((8, 2, BLOCK,...  47.7 us
    all_to_all x1, starting transfers between devices, shards(): lax.all_to_all(outbox, 'row', split_axis=0, concat_axis=0, tiled=True)  30.1 us
    all_gather x1, blocking collectives, shards(): lax.all_gather(dec_query, 'col', axis=1, tiled=True)  24.3 us
    all_to_all x1, starting transfers between devices, shards(): lax.all_to_all(reply_top, 'row', split_axis=0, concat_axis=0, tiled=True)  16.7 us
    all_to_all x1, waiting for transfers between devices, shards(): lax.all_to_all(outbox, 'row', split_axis=0, concat_axis=0, tiled=True)  16.2 us
    add x15, other arithmetic, join_partials(): weight_mass = first[1] * factor_one + second[1] * factor_two  10.4 us
  transfers between devices with their start and end apart: 7, of which 4 were waited for; matrix products, arithmetic and copies ran while one was open for 9% of the time, Pallas kernels for 47%

profile of v1, /device:TPU:1, one launch (start us, length us, event | category | flops | bytes accessed | tf_op | source)
XLA Modules:
  0.0 493.8 jit_solution(3568027148720630826)
XLA Ops:
  7.2 0.8 fusion.62
  8.0 1.4 scatter_fusion
  10.1 8.4 %all-to-all-start = ((s32[16,1,8]{2,1,0:T(1,128)}), s32[16,1,8]{2,1,0:T(1,128)}, u32[]{:S(2)}, u32[]{:S(2)}) async-start(s32[16,1,8]{2,1,0:T(1,128)} %copy.63), calls=%async_computation | async-start | bytes 16384 | tf_op jit(solution)/shard_map/all_to_all | solution.py:541
  18.6 0.7 reshape.218.gain
  20.0 1.2 copy-done.3
  21.2 0.9 copy-done.4
  22.2 0.9 copy-done.5
  23.1 47.7 %out_project.1 = (bf16[8,2,32,2048]{3,2,1,0:T(8,128)(2,1)S(1)}, bf16[32,2048]{1,0:T(8,128)(2,1)S(1)}) custom-call(bf16[512,256]{1,0:T(8,128)(2,1)S(1)} %copy-done.4, bf16[256,2048]{1,0:T(8,128)(2,1)S(1)} %copy-done.3, bf16[512,128]{1,0:T(8,128)(2,1)S(1)} %copy-done.5, bf16[1,2048]{1,0:T(2,128)(2,1)S(1)} %reshape.218.gain), custom_call_target="tpu_custom_call" | custom-call | tf_op jit(solution)/shard_map/out_project/pallas_call | solution.py:244
  70.8 1.3 copy-done.1
  72.1 0.7 copy-done.6
  72.8 0.7 copy-done.7
  73.6 184.6 %experts.1 = (bf16[8,2,32,2048]{3,2,1,0:T(8,128)(2,1)}, bf16[512,128]{1,0:T(8,128)(2,1)S(1)}) custom-call(bf16[512,2048]{1,0:T(8,128)(2,1)} %bitcast.144, s32[8,512]{1,0:T(8,128)S(1)} %bitcast.146, f32[8,512]{1,0:T(8,128)S(1)} %bitcast.147, bf16[2048,384]{1,0:T(8,128)(2,1)S(1)} %bitcast.145, bf16[2048,384]{1,0:T(8,128)(2,1)} %bitcast.149, ...), custom_call_target="tpu_custom_call" | custom-call | tf_op jit(solution)/shard_map/experts/pallas_call | solution.py:383
  258.2 2.1 multiply_reduce_fusion
  260.9 2.2 fusion.5
  263.2 1.4 convolution_convert_fusion.2
  265.3 0.7 add_convert_fusion
  266.0 0.8 convolution_convert_fusion
  267.5 1.0 multiply_cosine_fusion
  269.5 24.3 %all_gather.16 = bf16[8,4096]{1,0:T(8,128)(2,1)S(1)} all-gather(bf16[8,256]{1,0:T(8,128)(2,1)S(1)} %get-tuple-element.92), channel_id=1, replica_groups=mesh['row'=16,'col'=16] {'col'}, dimensions={1}, use_global_device_ids=true | all-gather | bytes 69632 | tf_op jit(solution)/shard_map/all_gather | solution.py:497
  293.7 1.1 broadcast_in_dim.50
  294.8 3.4 scatter_fusion.1
  298.2 30.1 %all-to-all-start.1 = ((bf16[16,8,4096]{2,1,0:T(8,128)(2,1)}), bf16[16,8,4096]{2,1,0:T(8,128)(2,1)S(1)}, u32[]{:S(2)}, u32[]{:S(2)}) async-start(bf16[16,8,4096]{2,1,0:T(8,128)(2,1)} %scatter_fusion.1), calls=%async_computation.1 | async-start | bytes 2097152 | tf_op jit(solution)/shard_map/all_to_all | solution.py:540
  328.8 0.7 reduce_sum.59
  329.5 0.7 broadcast_compare_fusion
  330.3 16.2 %all-to-all-done.1 = bf16[16,8,4096]{2,1,0:T(8,128)(2,1)S(1)} async-done(((bf16[16,8,4096]{2,1,0:T(8,128)(2,1)}), bf16[16,8,4096]{2,1,0:T(8,128)(2,1)S(1)}, u32[]{:S(2)}, u32[]{:S(2)}) %all-to-all-start.1) | async-done | bytes 1048608 | tf_op jit(solution)/shard_map/all_to_all | solution.py:540
  346.5 0.8 reduce_sum.60
  347.3 1.3 fusion.74
  348.6 2.3 convolution_bitcast_fusion
  350.9 0.9 fusion.13
  352.2 23.4 %all_gather.18 = f32[16,8,32]{2,1,0:T(8,128)S(1)} all-gather(f32[1,8,32]{2,1,0:T(8,128)S(1)} %all_gather_reshape.10), channel_id=1, replica_groups=mesh['row'=16,'col'=16] {'col'}, dimensions={0}, use_global_device_ids=true | all-gather | bytes 17408 | tf_op jit(solution)/shard_map/all_gather | solution.py:409
  376.3 26.6 %all_gather.17 = f32[16,8,32]{2,1,0:T(8,128)S(1)} all-gather(f32[1,8,32]{2,1,0:T(8,128)S(1)} %all_gather_reshape.9), channel_id=1, replica_groups=mesh['row'=16,'col'=16] {'col'}, dimensions={0}, use_global_device_ids=true | all-gather | bytes 17408 | tf_op jit(solution)/shard_map/all_gather | solution.py:409
  403.5 1.3 fusion.69
  405.1 1.0 copy.84
  406.2 1.8 fusion.68
  409.0 1.1 pad_maximum_fusion
  410.1 2.3 copy.62
  412.4 1.2 fusion.24
  414.3 0.9 fusion.71
  415.2 2.3 fusion.7
  418.4 1.5 constant_dynamic-slice_fusion.4
  420.5 0.7 fusion.41
  421.3 1.1 slice_bitcast_fusion
  422.9 13.2 %while.14 = (s32[]{:T(128)}, f32[8,32]{1,0:T(8,128)S(1)}, f32[8,32]{1,0:T(8,128)S(1)}, f32[8,32,128]{2,1,0:T(8,128)S(1)}, f32[15,8,32]{2,1,0:T(8,128)}, /*index=...) while((s32[]{:T(128)}, f32[8,32]{1,0:T(8,128)S(1)}, f32[8,32]{1,0:T(8,128)S(1)}, ...), condition=%wide.region_9.10_spmd, body=%wide.region_8.9_spmd.sunk | while | flops 99842 | bytes 403557 | solution.py:412
  422.9 0.7 fusion.83
  423.7 0.7 fusion.83
  424.6 0.7 fusion.83
  425.5 0.7 fusion.83
  426.4 0.7 fusion.83
  427.3 0.7 fusion.83
  428.1 0.7 fusion.83
  429.0 0.7 fusion.83
  429.9 0.7 fusion.83
  430.8 0.7 fusion.83
  431.7 0.7 fusion.83
  433.4 0.7 fusion.83
  434.3 0.7 fusion.83
  436.9 16.7 %all-to-all-start.3 = ((f32[16,8,2]{1,2,0:T(2,128)}), f32[16,8,2]{1,2,0:T(2,128)S(1)}, u32[]{:S(2)}, u32[]{:S(2)}) async-start(f32[16,8,2]{1,2,0:T(2,128)} %broadcast_in_dim.54), calls=%async_computation.3 | async-start | bytes 32768 | tf_op jit(solution)/shard_map/all_to_all | solution.py:571
  453.7 7.1 %all-to-all-done.3 = f32[16,8,2]{1,2,0:T(2,128)S(1)} async-done(((f32[16,8,2]{1,2,0:T(2,128)}), f32[16,8,2]{1,2,0:T(2,128)S(1)}, u32[]{:S(2)}, u32[]{:S(2)}) %all-to-all-start.3) | async-done | bytes 1056 | tf_op jit(solution)/shard_map/all_to_all | solution.py:571
  461.4 3.7 all-to-all-start.4
  465.9 6.6 %all-to-all-done.4 = f32[16,8,2]{1,2,0:T(2,128)S(1)} async-done(((f32[16,8,2]{1,2,0:T(2,128)}), f32[16,8,2]{1,2,0:T(2,128)S(1)}, u32[]{:S(2)}, u32[]{:S(2)}) %all-to-all-start.4) | async-done | bytes 1056 | tf_op jit(solution)/shard_map/all_to_all | solution.py:572
  473.2 3.7 all-to-all-start.2
  477.6 0.7 multiply_add_fusion
  478.3 6.2 %all-to-all-done.2 = f32[16,8,2,128]{3,2,1,0:T(2,128)S(1)} async-done(((f32[16,8,2,128]{3,2,1,0:T(2,128)}), f32[16,8,2,128]{3,2,1,0:T(2,128)S(1)}, u32[]{:S(2)}, u32[]{:S(2)}) %all-to-all-start.2) | async-done | bytes 131104 | tf_op jit(solution)/shard_map/all_to_all | solution.py:573
  485.5 0.8 copy.77
  (96 shorter events, 20.0 us)
Async XLA Ops:
  7.2 258.9 %copy-start = (bf16[2048,256]{1,0:T(8,128)(2,1)S(1)}, bf16[2048,256]{1,0:T(8,128)(2,1)}, u32[]{:S(2)}) copy-start(bf16[2048,256]{1,0:T(8,128)(2,1)} %param.29) | copy-start | bytes 3145732
  7.2 64.9 %copy-start.2 = (bf16[1,2048,384]{2,1,0:T(8,128)(2,1)S(1)}, bf16[1,2048,384]{2,1,0:T(8,128)(2,1)}, u32[]{:S(2)}) copy-start(bf16[1,2048,384]{2,1,0:T(8,128)(2,1)} %param.26) | copy-start | bytes 4718596
  10.1 288.0 %all-to-all-start = ((s32[16,1,8]{2,1,0:T(1,128)}), s32[16,1,8]{2,1,0:T(1,128)}, u32[]{:S(2)}, u32[]{:S(2)}) async-start(s32[16,1,8]{2,1,0:T(1,128)} %copy.63), calls=%async_computation | async-start | bytes 16384 | tf_op jit(solution)/shard_map/all_to_all | solution.py:541
  18.6 384.9 %all-gather.3.cloned.1.call-start = ((), (), s32[]{:S(2)}) async-start(), calls=%async_computation.5 | async-start | bytes 1114112 | tf_op jit(solution)/shard_map/all_gather | solution.py:496
  20.0 1.2 copy-start.3
  21.2 0.9 copy-start.4
  22.2 0.9 copy-start.5
  70.8 1.3 copy-start.1
  72.1 0.7 copy-start.6
  72.8 0.7 copy-start.7
  260.9 2.2 copy-start.10
  263.1 2.0 copy-start.13
  266.8 0.7 copy-start.15
  294.8 52.5 %copy-start.9 = (bf16[8,64,512]{2,1,0:T(8,128)(2,1)S(1)}, bf16[8,64,512]{2,1,0:T(8,128)(2,1)}, u32[]{:S(2)}) copy-start(bf16[8,64,512]{2,1,0:T(8,128)(2,1)} %param.34) | copy-start | bytes 1572868
  298.2 48.3 %all-to-all-start.1 = ((bf16[16,8,4096]{2,1,0:T(8,128)(2,1)}), bf16[16,8,4096]{2,1,0:T(8,128)(2,1)S(1)}, u32[]{:S(2)}, u32[]{:S(2)}) async-start(bf16[16,8,4096]{2,1,0:T(8,128)(2,1)} %scatter_fusion.1), calls=%async_computation.1 | async-start | bytes 2097152 | tf_op jit(solution)/shard_map/all_to_all | solution.py:540
  328.3 93.0 %all-gather.5.cloned.1.call-start = ((), (), s32[]{:S(2)}) async-start(), calls=%async_computation.6 | async-start | bytes 2228224 | tf_op jit(solution)/shard_map/all_gather | solution.py:409
  408.0 1.0 copy-start.8
  410.1 4.2 copy-start.11
  413.6 0.7 copy-start.12
  415.2 5.3 %copy-start.14 = (bf16[8,2,128]{2,0,1:T(8,128)(2,1)S(1)}, bf16[8,2,128]{2,0,1:T(8,128)(2,1)}, u32[]{:S(2)}) copy-start(bf16[8,2,128]{2,0,1:T(8,128)(2,1)} %get-tuple-element.91) | copy-start | bytes 12292
  421.3 1.6 slice-start
  436.9 24.0 %all-to-all-start.3 = ((f32[16,8,2]{1,2,0:T(2,128)}), f32[16,8,2]{1,2,0:T(2,128)S(1)}, u32[]{:S(2)}, u32[]{:S(2)}) async-start(f32[16,8,2]{1,2,0:T(2,128)} %broadcast_in_dim.54), calls=%async_computation.3 | async-start | bytes 32768 | tf_op jit(solution)/shard_map/all_to_all | solution.py:571
  461.4 11.0 %all-to-all-start.4 = ((f32[16,8,2]{1,2,0:T(2,128)}), f32[16,8,2]{1,2,0:T(2,128)S(1)}, u32[]{:S(2)}, u32[]{:S(2)}) async-start(f32[16,8,2]{1,2,0:T(2,128)} %broadcast_in_dim.55), calls=%async_computation.4 | async-start | bytes 32768 | tf_op jit(solution)/shard_map/all_to_all | solution.py:572
  473.2 11.4 %all-to-all-start.2 = ((f32[16,8,2,128]{3,2,1,0:T(2,128)}), f32[16,8,2,128]{3,2,1,0:T(2,128)S(1)}, u32[]{:S(2)}, u32[]{:S(2)}) async-start(f32[16,8,2,128]{3,2,1,0:T(2,128)} %broadcast_in_dim.53), calls=%async_computation.2 | async-start | bytes 262144 | tf_op jit(solution)/shard_map/all_to_all | solution.py:573
Sparse Core Ops, SparseCore 0:
  264.7 79.6 all-gather.2
  351.0 68.7 all-gather.4

commit v2 on v1

--- a/solution.py
+++ b/solution.py
@@ -259,12 +259,13 @@
 
 
 GROUPS = (8, 12, 4, 0)
+TABLE_SEMS = 32 + 2 * RING_SEMS
 
 
 def expert_kernel(
-    normed, routes, scores, w_gate, w_up, w_down, mid, full, share,
+    normed, routes, scores, w_gate, w_up, w_down, mid, table, full, share, tables,
     blocks, y_left, up_left, down_left, up_right, down_right, y_right,
-    going, coming, back, total, weights, send, recv,
+    going, coming, back, total, weights, listed, send, recv,
 ):
     row = lax.axis_index("row")
     place = around()
@@ -304,6 +305,11 @@
     pl.semaphore_wait(barrier, 18)
     started = []
     arrivals = {}
+    lists = []
+    for o in range(1, 16):
+        copy = remote(table, listed.at[o], send, recv, TABLE_SEMS + o, partner(o, 1))
+        copy.start()
+        lists.append(copy)
     for group in GROUPS:
         picks = []
         for o in range(group, group + 4):
@@ -345,6 +351,12 @@
             started.append(copy)
             returns[o] = copy
     back[0] = coming[0]
+    for copy in lists:
+        copy.wait_recv()
+    known = table[...]
+    for o in range(1, 16):
+        known = known + listed[o]
+    tables[...] = known
     for index, group in enumerate(GROUPS[::-1]):
         for o in range(max(group, 1), group + 4):
             returns[o].wait_recv()
@@ -370,24 +382,25 @@
     )
     full[z, y, :, LEFT] = (mid[:, :HALF_D].astype(jnp.float32) + left).astype(jnp.bfloat16)
     full[z, y, :, RIGHT] = (mid[:, HALF_D:].astype(jnp.float32) + right).astype(jnp.bfloat16)
-    started = started + ring + gather_blocks(place, full, send, recv, 32 + RING_SEMS)
+    started = started + lists + ring + gather_blocks(place, full, send, recv, 32 + RING_SEMS)
     own = pl.ds(pl.multiple_of((z * 2 + y) * 128, 128), 128)
     share[...] = full[:, :, :, own].reshape(ROWS, 128)
     for copy in started:
         copy.wait_send()
 
 
-def experts(normed, routes, scores, w_gate, w_up, w_down, mid):
+def experts(normed, routes, scores, w_gate, w_up, w_down, mid, table):
     vmem = pl.BlockSpec(memory_space=pltpu.VMEM)
-    sems = 32 + 2 * RING_SEMS
+    sems = TABLE_SEMS + 16
     return pl.pallas_call(
         expert_kernel,
         out_shape=(
             jax.ShapeDtypeStruct((8, 2, BLOCK, D), jnp.bfloat16),
             jax.ShapeDtypeStruct((ROWS, 128), jnp.bfloat16),
+            jax.ShapeDtypeStruct((8, 128), jnp.int32),
         ),
-        in_specs=[vmem] * 7,
-        out_specs=(vmem, vmem),
+        in_specs=[vmem] * 8,
+        out_specs=(vmem, vmem, vmem),
         scratch_shapes=ring_scratch()
         + [
             pltpu.VMEM((16, CAP, D), jnp.bfloat16),
@@ -395,6 +408,7 @@
             pltpu.VMEM((16, CAP, D), jnp.bfloat16),
             pltpu.VMEM((ROWS, D), jnp.float32),
             pltpu.VMEM((16 * CAP, ROWS), jnp.bfloat16),
+            pltpu.VMEM((16, 8, 128), jnp.int32),
             pltpu.SemaphoreType.DMA((sems,)),
             pltpu.SemaphoreType.DMA((sems,)),
         ],
@@ -402,48 +416,242 @@
             collective_id=1, has_side_effects=True, vmem_limit_bytes=52 << 20
         ),
         name="experts",
-    )(normed, routes, scores, w_gate, w_up, w_down, mid)
-
-
-def merged_2(value, axis, join):
-    pieces = jax.tree.map(lambda part: lax.all_gather(part, axis), value)
-    head = jax.tree.map(lambda part: part[0], pieces)
-    tail = jax.tree.map(lambda part: part[1:], pieces)
-    running, _ = lax.scan(lambda running, share: (join(running, share), None), head, tail)
-    return running
-
-
-def rms_norm(hidden, gain_vector):
-    values = hidden.astype(jnp.float32)
-    inverse = lax.rsqrt(jnp.mean(values * values, axis=-1, keepdims=True) + EPSILON)
-    return (values * inverse * gain_vector.astype(jnp.float32)).astype(jnp.bfloat16)
-
-
-def rotate(values, positions):
-    head_width = values.shape[-1]
-    half_width = head_width // 2
-    indices = jnp.arange(half_width).astype(jnp.float32)
-    inverse = ROPE_THETA ** (-2.0 * indices / head_width)
-    angles = positions.astype(jnp.float32)[:, None] * inverse[None, :]
-    cosine = jnp.concatenate([jnp.cos(angles), jnp.cos(angles)], axis=-1)[:, None, :]
-    sine_part = jnp.concatenate([jnp.sin(angles), jnp.sin(angles)], axis=-1)[:, None, :]
-    floats = values.astype(jnp.float32)
-    turned = jnp.concatenate([-floats[..., half_width:], floats[..., :half_width]], axis=-1)
-    return (floats * cosine + turned * sine_part).astype(jnp.bfloat16)
-
-
-def segment_positions(segment_rows):
-    earlier = jnp.sum((segment_rows[None, :] < segment_rows[:, None]).astype(jnp.int32), axis=1)
-    return jnp.arange(segment_rows.shape[0], dtype=jnp.int32) - earlier
-
-
-def join_partials(first, second):
-    highest = jnp.maximum(first[0], second[0])
-    factor_one = jnp.exp(first[0] - highest)
-    factor_two = jnp.exp(second[0] - highest)
-    weight_mass = first[1] * factor_one + second[1] * factor_two
-    accum_out = first[2] * factor_one[..., None] + second[2] * factor_two[..., None]
-    return (highest, weight_mass, accum_out)
+    )(normed, routes, scores, w_gate, w_up, w_down, mid, table)
+
+
+SCALE = HD ** (-0.5)
+PACK = 384
+
+
+def turn(value, cosine, sine):
+    return value * cosine + pltpu.roll(value, HD // 2, value.ndim - 1) * sine
+
+
+def stats_of(top, mass, lane):
+    return jnp.where(
+        lane == 0, top[0], jnp.where(lane == 1, top[1], jnp.where(lane == 2, mass[0], mass[1]))
+    )
+
+
+def attend_kernel(
+    full, gain, w_query, w_keyval, cosine, sine, segment_column, segment_row, holders, tables,
+    cache_keys, cache_values, new_cache, attention,
+    x_in, query, pieces, keys, values, own_query, all_query, slot_query, slots_query,
+    parts, parts_in, reply, replies, send, recv,
+):
+    row = lax.axis_index("row")
+    col = lax.axis_index("col")
+    quarter = lax.rem(col, 4)
+    first = col - quarter
+
+    def along_row(o):
+        return (lax.rem(row + o, 16), col)
+
+    def along_col(o):
+        return (row, lax.rem(col + o, 16))
+
+    barrier = greet([along_row(o) for o in range(1, 16)] + [along_col(o) for o in range(1, 16)])
+    started = []
+
+    def go(src, dst, index, device):
+        copy = remote(src, dst, send, recv, index, device)
+        copy.start()
+        started.append(copy)
+        return copy
+
+    gains = gain[...].astype(jnp.float32)
+
+    def norm(value):
+        value = value.astype(jnp.float32)
+        inverse = lax.rsqrt(jnp.mean(value * value, axis=-1, keepdims=True) + EPSILON)
+        return (value * inverse * gains).astype(jnp.bfloat16)
+
+    early = jnp.dot(norm(full[:16, :]), w_query[...], preferred_element_type=jnp.float32)
+    early = early.astype(jnp.bfloat16).astype(jnp.float32)
+    for head in range(2):
+        span = pl.ds(head * HD, HD)
+        turned = turn(early[:, head * HD : (head + 1) * HD], cosine[:16, :], sine[:16, :])
+        own_query[:, span] = turned.astype(jnp.bfloat16).astype(jnp.float32)[:8]
+    all_query[row] = own_query[...]
+    pl.semaphore_wait(barrier, 30)
+    asks = [go(own_query, all_query.at[row], o, along_row(o)) for o in range(1, 16)]
+    for tile in range(0, ROWS, 64):
+        x_in[tile : tile + 64, :] = norm(full[tile : tile + 64, :])
+    keyval = jnp.dot(x_in[...], w_keyval[...], preferred_element_type=jnp.float32).astype(jnp.bfloat16)
+    pieces[quarter] = jnp.concatenate([keyval[: ROWS // 2], keyval[ROWS // 2 :]], axis=1)
+    shares = [
+        go(pieces.at[quarter], pieces.at[quarter], 16 + o, (row, first + lax.rem(quarter + o, 4)))
+        for o in range(1, 4)
+    ]
+    for copy in asks:
+        copy.wait_recv()
+    held = (
+        tables[0:1, :] == row * 8 + lax.broadcasted_iota(jnp.int32, (8, 128), 0)
+    )
+    length = jnp.sum(jnp.where(held, tables[1:2, :], 0), axis=1, keepdims=True)
+    slot_query[...] = jnp.dot(
+        jnp.where(held, 1.0, 0.0).astype(jnp.bfloat16),
+        all_query[...].reshape(128, 2 * HD).astype(jnp.bfloat16),
+        preferred_element_type=jnp.float32,
+    )
+    slots_query[col] = slot_query[...]
+    tells = [go(slot_query, slots_query.at[col], 20 + o, along_col(o)) for o in range(1, 16)]
+    for head in range(2):
+        span = pl.ds(head * HD, HD)
+        value = jnp.dot(x_in[...], w_query[:, span], preferred_element_type=jnp.float32)
+        value = value.astype(jnp.bfloat16).astype(jnp.float32)
+        query[:, span] = turn(value, cosine[...], sine[...]).astype(jnp.bfloat16)
+    for copy in tells:
+        copy.wait_recv()
+    group = lax.rem(lax.broadcasted_iota(jnp.int32, (32, 4 * HD), 0), 16) // 4
+    matched = group == lax.broadcasted_iota(jnp.int32, (32, 4 * HD), 1) // HD
+    spot = col * 64 + lax.broadcasted_iota(jnp.int32, (32, 64), 1)
+    lane = lax.broadcasted_iota(jnp.int32, (16, HD), 1)
+    for slot in range(8):
+        asked = slots_query[:, slot, :]
+        asked = jnp.concatenate([asked[:, :HD], asked[:, HD:]], axis=0)
+        asked = jnp.where(matched, jnp.concatenate([asked] * 4, axis=1), 0.0).astype(jnp.bfloat16)
+        scores = SCALE * lax.dot_general(
+            asked, cache_keys[slot], (((1,), (1,)), ((), ())), preferred_element_type=jnp.float32
+        )
+        valid = spot < length[slot : slot + 1, :]
+        scores = jnp.where(valid, scores, NEGATIVE)
+        top = jnp.max(scores, axis=1, keepdims=True)
+        grown = jnp.where(valid, jnp.exp(scores - top), 0.0)
+        mass = jnp.sum(grown, axis=1, keepdims=True)
+        blend = jnp.dot(grown.astype(jnp.bfloat16), cache_values[slot], preferred_element_type=jnp.float32)
+        blend = jnp.where(matched, blend, 0.0)
+        blend = blend[:, :HD] + blend[:, HD : 2 * HD] + blend[:, 2 * HD : 3 * HD] + blend[:, 3 * HD :]
+        parts[:, slot, :HD] = blend[:16]
+        parts[:, slot, HD : 2 * HD] = blend[16:]
+        parts[:, slot, 2 * HD :] = stats_of((top[:16], top[16:]), (mass[:16], mass[16:]), lane)
+    parts_in[0] = parts[col]
+    sums = [
+        go(parts.at[lax.rem(col + o, 16)], parts_in.at[o], 36 + o, along_col(o)) for o in range(1, 16)
+    ]
+    for copy in shares:
+        copy.wait_recv()
+
+    def piece(index):
+        value = pieces[index]
+        return jnp.concatenate([value[:, : HD // 2], value[:, HD // 2 :]], axis=0)
+
+    quarters = [piece(index) for index in range(4)]
+    key = jnp.concatenate(quarters[:2], axis=1).astype(jnp.float32)
+    keys[...] = turn(key, cosine[...], sine[...]).astype(jnp.bfloat16)
+    values[...] = jnp.concatenate(quarters[2:], axis=1)
+    new_cache[...] = jnp.where(
+        quarter == 0,
+        keys[:, : HD // 2],
+        jnp.where(
+            quarter == 1,
+            keys[:, HD // 2 :],
+            jnp.where(quarter == 2, values[:, : HD // 2], values[:, HD // 2 :]),
+        ),
+    )
+
+    def prompt(head):
+        span = pl.ds(head * HD, HD)
+        for tile in range(0, ROWS, 128):
+            reach = tile + 128
+            scores = SCALE * lax.dot_general(
+                query[tile:reach, span], keys[:reach, :], (((1,), (1,)), ((), ())),
+                preferred_element_type=jnp.float32,
+            )
+            allowed = (segment_column[tile:reach, :] == segment_row[:, :reach]) & (
+                lax.broadcasted_iota(jnp.int32, (128, reach), 1)
+                <= lax.broadcasted_iota(jnp.int32, (128, reach), 0) + tile
+            )
+            scores = jnp.where(allowed, scores, NEGATIVE)
+            grown = jnp.exp(scores - jnp.max(scores, axis=1, keepdims=True))
+            chance = (grown / jnp.sum(grown, axis=1, keepdims=True)).astype(jnp.bfloat16)
+            attention[tile:reach, span] = jnp.dot(
+                chance, values[:reach, :], preferred_element_type=jnp.float32
+            ).astype(jnp.bfloat16)
+
+    prompt(0)
+    for copy in sums:
+        copy.wait_recv()
+    tops, masses = [], []
+    for head in range(2):
+        top = parts_in[:, :, 2 * HD + head : 2 * HD + head + 1]
+        mass = parts_in[:, :, 2 * HD + 2 + head : 2 * HD + 3 + head]
+        highest = jnp.max(top, axis=0)
+        factor = jnp.exp(top - highest[None])
+        span = pl.ds(head * HD, HD)
+        reply[:, span] = jnp.sum(parts_in[:, :, span] * factor, axis=0)
+        tops.append(highest)
+        masses.append(jnp.sum(mass * factor, axis=0))
+    reply[:, 2 * HD :] = stats_of(tops, masses, lane[:8])
+    replies[row] = reply[...]
+    backs = [go(reply, replies.at[row], 52 + o, along_row(o)) for o in range(1, 16)]
+    prompt(1)
+    for copy in backs:
+        copy.wait_recv()
+    mine = jnp.where(holders[...] == lax.broadcasted_iota(jnp.int32, (8, 128), 1), 1.0, 0.0)
+    got = jnp.dot(
+        mine,
+        replies[...].reshape(128, PACK),
+        preferred_element_type=jnp.float32,
+        precision=lax.Precision.HIGHEST,
+    )
+    own_key = keys[:16, :].astype(jnp.float32)[:8]
+    own_value = values[:16, :].astype(jnp.float32)[:8]
+    for head in range(2):
+        span = pl.ds(head * HD, HD)
+        own = SCALE * jnp.sum(own_query[:, span] * own_key, axis=1, keepdims=True)
+        top = got[:, 2 * HD + head : 2 * HD + head + 1]
+        mass = got[:, 2 * HD + 2 + head : 2 * HD + 3 + head]
+        highest = jnp.maximum(top, own)
+        theirs = jnp.exp(top - highest)
+        ours = jnp.exp(own - highest)
+        result = (got[:, head * HD : (head + 1) * HD] * theirs + own_value * ours) / (mass * theirs + ours)
+        result = jnp.concatenate([result, result], axis=0)
+        decoded = lax.broadcasted_iota(jnp.int32, (16, HD), 0) < 8
+        attention[:16, span] = jnp.where(
+            decoded, result, attention[:16, span].astype(jnp.float32)
+        ).astype(jnp.bfloat16)
+    for copy in started:
+        copy.wait_send()
+
+
+def attend(full, gain, w_query, w_keyval, cosine, sine, segments, holders, tables, cache_keys, cache_values):
+    vmem = pl.BlockSpec(memory_space=pltpu.VMEM)
+    f32, bf16 = jnp.float32, jnp.bfloat16
+    return pl.pallas_call(
+        attend_kernel,
+        out_shape=(
+            jax.ShapeDtypeStruct((ROWS, 64), bf16),
+            jax.ShapeDtypeStruct((ROWS, 2 * HD), bf16),
+        ),
+        in_specs=[vmem] * 12,
+        out_specs=(vmem, vmem),
+        scratch_shapes=[
+            pltpu.VMEM((ROWS, D), bf16),
+            pltpu.VMEM((ROWS, 2 * HD), bf16),
+            pltpu.VMEM((4, ROWS // 2, HD), bf16),
+            pltpu.VMEM((ROWS, HD), bf16),
+            pltpu.VMEM((ROWS, HD), bf16),
+            pltpu.VMEM((8, 2 * HD), f32),
+            pltpu.VMEM((16, 8, 2 * HD), f32),
+            pltpu.VMEM((8, 2 * HD), f32),
+            pltpu.VMEM((16, 8, 2 * HD), f32),
+            pltpu.VMEM((16, 8, PACK), f32),
+            pltpu.VMEM((16, 8, PACK), f32),
+            pltpu.VMEM((8, PACK), f32),
+            pltpu.VMEM((16, 8, PACK), f32),
+            pltpu.SemaphoreType.DMA((68,)),
+            pltpu.SemaphoreType.DMA((68,)),
+        ],
+        compiler_params=pltpu.CompilerParams(
+            collective_id=2, has_side_effects=True, vmem_limit_bytes=48 << 20
+        ),
+        name="attend",
+    )(
+        full, gain.reshape(1, D), w_query, w_keyval, cosine, sine,
+        segments.reshape(ROWS, 1), segments.reshape(1, ROWS), holders.reshape(8, 1), tables,
+        cache_keys, cache_values,
+    )
 
 
 def shards(
@@ -465,135 +673,29 @@
     cache_keys,
     cache_values,
 ):
-    col_index = lax.axis_index("col")
-    col_count = lax.axis_size("col")
-    row_count = lax.axis_size("row")
-    tok_rows = attn_context.shape[0]
+    row = lax.axis_index("row")
+    segment = segment_ids[0]
+    earlier = jnp.sum((segment[None, :] < segment[:, None]).astype(jnp.int32), axis=1)
+    position = jnp.concatenate([cache_lengths, jnp.arange(segment.shape[0], dtype=jnp.int32) - earlier])
+    indices = jnp.arange(HD // 2).astype(jnp.float32)
+    angles = position.astype(jnp.float32)[:, None] * (ROPE_THETA ** (-2.0 * indices / HD))[None, :]
+    cosine, sine = jnp.cos(angles), jnp.sin(angles)
+    cosine = jnp.concatenate([cosine, cosine], axis=1)
+    sine = jnp.concatenate([-sine, sine], axis=1)
+    segments = jnp.concatenate([jnp.full((8,), -1, jnp.int32), segment])
+    table = jnp.stack([holders, cache_lengths])
+    table = jnp.pad(table, ((0, 6), (0, 0)))
+    table = jnp.where(
+        jnp.arange(128, dtype=jnp.int32)[None, :] // 8 == row, jnp.tile(table, (1, 16)), 0
+    )
     normed, mid = out_project(attn_context, w_out, residual, gain_post)
-    full, hidden_out = experts(
-        normed.reshape(tok_rows, D),
-        routes.T,
-        router_scores.T,
-        w_gate[0],
-        w_up[0],
-        w_down[0],
-        mid,
-    )
-    x_in = rms_norm(full.reshape(tok_rows, D), gain_input)
-    heads_local = QH // col_count
-    dec_count = cache_lengths.shape[0]
-    score_scale = HD ** (-0.5)
-    query_local = (
-        jnp.dot(x_in, w_query, preferred_element_type=jnp.float32)
-        .astype(jnp.bfloat16)
-        .reshape(tok_rows, heads_local, HD)
-    )
-    keyval_local = jnp.dot(x_in, w_keyval, preferred_element_type=jnp.float32).astype(jnp.bfloat16)
-    position = jnp.concatenate([cache_lengths, segment_positions(segment_ids[0])], axis=0)
-    query_rot = rotate(query_local, position)
-    dec_query = query_rot[:dec_count].reshape(dec_count, heads_local * HD)
-    keyval_all, payload = (
-        lax.all_gather(keyval_local, "col", axis=1, tiled=True),
-        lax.all_gather(dec_query, "col", axis=1, tiled=True),
-    )
-    keyval_heads = keyval_all.reshape(tok_rows, KVH, 2, HD)
-    key_rot = rotate(keyval_heads[:, :, 0, :], position)
-    value_rows = keyval_heads[:, :, 1, :]
-    cache_full = jnp.stack([key_rot, value_rows], axis=2).reshape(tok_rows, 2 * KVH * HD)
-    cache_share = cache_full.shape[1] // col_count
-    new_cache = lax.dynamic_slice_in_dim(cache_full, col_index * cache_share, cache_share, 1)
-    head_kv = col_index * heads_local // (QH // KVH)
-    my_keys = lax.dynamic_index_in_dim(key_rot, head_kv, 1, keepdims=False)
-    my_values = lax.dynamic_index_in_dim(value_rows, head_kv, 1, keepdims=False)
-    prompt_query = query_rot[dec_count:]
-    prompt_keys = my_keys[dec_count:]
-    prompt_values = my_values[dec_count:]
-    prompt_rows = prompt_query.shape[0]
-    scores = (
-        jnp.einsum("ihd,jd->hij", prompt_query, prompt_keys, preferred_element_type=jnp.float32)
-        * score_scale
-    )
-    ordinal = jnp.arange(prompt_rows)
-    segment_rows = segment_ids[0]
-    allowed = (segment_rows[:, None] == segment_rows[None, :]) & (
-        ordinal[None, :] <= ordinal[:, None]
-    )
-    scores = jnp.where(allowed[None, :, :], scores, NEGATIVE)
-    highest = jnp.max(scores, axis=-1, keepdims=True)
-    exponent = jnp.exp(scores - highest)
-    probability = (exponent / jnp.sum(exponent, axis=-1, keepdims=True)).astype(jnp.bfloat16)
-    prompt_out = jnp.einsum(
-        "hij,jd->ihd", probability, prompt_values, preferred_element_type=jnp.float32
-    )
-    prompt_out = prompt_out.astype(jnp.bfloat16).reshape(prompt_rows, heads_local * HD)
-    holder_dev = holders // dec_count
-    holder_slot = holders % dec_count
-    outbox = (
-        jnp.zeros((row_count, dec_count, payload.shape[1]), jnp.bfloat16)
-        .at[holder_dev, holder_slot]
-        .set(payload)
-    )
-    length_box = (
-        jnp.zeros((row_count, dec_count), jnp.int32).at[holder_dev, holder_slot].set(cache_lengths)
-    )
-    inbox, length_in = (
-        lax.all_to_all(outbox, "row", split_axis=0, concat_axis=0, tiled=True),
-        lax.all_to_all(length_box, "row", split_axis=0, concat_axis=0, tiled=True),
-    )
-    slot_query = jnp.sum(inbox.astype(jnp.float32), axis=0).astype(jnp.bfloat16)
-    slot_length = jnp.sum(length_in, axis=0)
-    span_len = cache_keys.shape[1]
-    span_start = col_index * span_len
-    grouped = slot_query.reshape(dec_count, KVH, QH // KVH, HD)
-    held_keys = cache_keys.reshape(dec_count, span_len, KVH, HD)
-    held_values = cache_values.reshape(dec_count, span_len, KVH, HD).astype(jnp.float32)
-    held_scores = (
-        jnp.einsum("sgqd,stgd->sgqt", grouped, held_keys, preferred_element_type=jnp.float32)
-        * score_scale
-    )
-    valid = ((span_start + jnp.arange(span_len))[None, :] < slot_length[:, None])[:, None, None, :]
-    held_scores = jnp.where(valid, held_scores, NEGATIVE)
-    score_top = jnp.max(held_scores, axis=-1)
-    held_exp = jnp.where(valid, jnp.exp(held_scores - score_top[..., None]), 0.0)
-    weight_mass = jnp.sum(held_exp, axis=-1).reshape(dec_count, QH)
-    accum_out = jnp.einsum(
-        "sgqt,stgd->sgqd", held_exp, held_values, precision=lax.Precision.HIGHEST
-    ).reshape(dec_count, QH, HD)
-    score_top = score_top.reshape(dec_count, QH)
-    merged = merged_2((score_top, weight_mass, accum_out), "col", join_partials)
-    part_top = lax.dynamic_slice_in_dim(merged[0], col_index * heads_local, heads_local, 1)
-    part_mass = lax.dynamic_slice_in_dim(merged[1], col_index * heads_local, heads_local, 1)
-    part_accum = lax.dynamic_slice_in_dim(merged[2], col_index * heads_local, heads_local, 1)
-    reply_top = jnp.broadcast_to(part_top[None], (row_count,) + part_top.shape)
-    reply_mass = jnp.broadcast_to(part_mass[None], (row_count,) + part_mass.shape)
-    reply_accum = jnp.broadcast_to(part_accum[None], (row_count,) + part_accum.shape)
-    back_top, back_mass, back_accum = (
-        lax.all_to_all(reply_top, "row", split_axis=0, concat_axis=0, tiled=True),
-        lax.all_to_all(reply_mass, "row", split_axis=0, concat_axis=0, tiled=True),
-        lax.all_to_all(reply_accum, "row", split_axis=0, concat_axis=0, tiled=True),
-    )
-    remote_top = back_top[holder_dev, holder_slot]
-    remote_mass = back_mass[holder_dev, holder_slot]
-    remote_accum = back_accum[holder_dev, holder_slot]
-    own_query = query_rot[:dec_count].astype(jnp.float32)
-    own_key = my_keys[:dec_count].astype(jnp.float32)
-    own_value = my_values[:dec_count].astype(jnp.float32)
-    own_score = (
-        jnp.einsum("shd,sd->sh", own_query, own_key, precision=lax.Precision.HIGHEST) * score_scale
-    )
-    final_top = jnp.maximum(remote_top, own_score)
-    remote_factor = jnp.exp(remote_top - final_top)
-    own_factor = jnp.exp(own_score - final_top)
-    numerator = (
-        remote_accum * remote_factor[..., None] + own_factor[..., None] * own_value[:, None, :]
-    )
-    denominator = remote_mass * remote_factor + own_factor
-    decode_out = (
-        (numerator / denominator[..., None])
-        .reshape(dec_count, heads_local * HD)
-        .astype(jnp.bfloat16)
-    )
-    attention_out = jnp.concatenate([decode_out, prompt_out], axis=0)
+    full, hidden_out, tables = experts(
+        normed.reshape(ROWS, D), routes.T, router_scores.T, w_gate[0], w_up[0], w_down[0], mid, table
+    )
+    new_cache, attention_out = attend(
+        full.reshape(ROWS, D), gain_input, w_query, w_keyval, cosine, sine, segments, holders, tables,
+        cache_keys, cache_values,
+    )
     return (hidden_out, new_cache, attention_out)
 
 

time: 496 us -> 304 us (0.61)
  blocking collectives: 74.3 us -> 0 us
  starting transfers between devices: 62.6 us -> 0 us
  Pallas kernels: 232 us -> 285 us
  waiting for transfers between devices: 36.2 us -> 0 us
  other arithmetic: 31.8 us -> 2.23 us
  local copies, waits for them, and re-layouts: 32.3 us -> 15.2 us
  between operations: 14.3 us -> 0.88 us
  matrix products: 9.72 us -> 0 us
    all_gather x3 -> x0, blocking collectives: 74.3 us -> none  [the longest x2 50 us: merged_2(): pieces = jax.tree.map(lambda part: lax.all_gather(part, axis), value)]
    all_to_all x5 -> x0, starting transfers between devices: 62.6 us -> none  [the longest x1 30.1 us: shards(): lax.all_to_all(outbox, 'row', split_axis=0, concat_axis=0, tiled=True)]
    pallas_call x0 -> x1, Pallas kernels: none -> 50.7 us  [attend(): pl.pallas_call(attend_kernel, out_shape=(jax.ShapeDtypeStruct((ROWS, 64),...]
    all_to_all x5 -> x0, waiting for transfers between devices: 36.2 us -> none  [the longest x1 16.2 us: shards(): lax.all_to_all(outbox, 'row', split_axis=0, concat_axis=0, tiled=True)]
    add x32 -> x0, other arithmetic: 14.2 us -> none  [the longest x15 10.4 us: join_partials(): weight_mass = first[1] * factor_one + second[1] * factor_two]
    dot_general x6 -> x0, matrix products: 8.77 us -> none  [the longest x1 2.31 us: shards(): jnp.einsum('hij,jd->ihd', probability, prompt_values, preferred_element_t...]
    convert_element_type x9 -> x1, other arithmetic: 6.27 us -> 0.08 us  [shards(): position.astype(jnp.float32)[:, None]]
    unnamed x36 -> x44, local copies, waits for them, and re-layouts: 10.2 us -> 14 us
  transfers between devices with their start and end apart: 7 -> 0, of which waited for: 4 -> 0; matrix products, arithmetic and copies ran while one was open for 9% -> 0% of each run, Pallas kernels for 47% -> 0%
where the time goes in v2:
time: 304 us
  Pallas kernels  285 us (94%)
  local copies, waits for them, and re-layouts  15.2 us (5%)
    pallas_call x1, Pallas kernels, experts(): pl.pallas_call(expert_kernel, out_shape=(jax.ShapeDtypeStruct((8, 2, BLOC...  188 us
    pallas_call x1, Pallas kernels, attend(): pl.pallas_call(attend_kernel, out_shape=(jax.ShapeDtypeStruct((ROWS, 64),...  50.7 us
    pallas_call x1, Pallas kernels, out_project(): pl.pallas_call(out_kernel, out_shape=(jax.ShapeDtypeStruct((8, 2, BLOCK,...  46.8 us
    unnamed x44, local copies, waits for them, and re-layouts  14 us

profile of v2, /device:TPU:1, one launch (start us, length us, event | category | flops | bytes accessed | tf_op | source)
XLA Modules:
  0.0 303.5 jit_solution(8318273657652420359)
XLA Ops:
  0.6 0.0 copy-start.2
  0.6 0.8 reshape.92.gain
  1.5 0.0 copy-start.4
  1.5 1.2 copy-done.4
  2.7 0.0 copy-start.8
  2.7 0.9 copy-done.8
  3.6 0.0 copy-start.10
  3.6 0.9 copy-done.10
  4.5 0.0 copy-start.11
  4.5 0.0 copy-start.12
  4.5 46.8 %out_project.1 = (bf16[8,2,32,2048]{3,2,1,0:T(8,128)(2,1)S(1)}, bf16[32,2048]{1,0:T(8,128)(2,1)S(1)}) custom-call(bf16[512,256]{1,0:T(8,128)(2,1)S(1)} %copy-done.8, bf16[256,2048]{1,0:T(8,128)(2,1)S(1)} %copy-done.4, bf16[512,128]{1,0:T(8,128)(2,1)S(1)} %copy-done.10, bf16[1,2048]{1,0:T(2,128)(2,1)S(1)} %reshape.92.gain), custom_call_target="tpu_custom_call" | custom-call | tf_op jit(solution)/shard_map/out_project/pallas_call | solution.py:244
  51.3 0.0 copy-start.1
  51.3 1.3 copy-done.1
  52.6 0.7 pad_add_fusion
  53.3 0.1 tile.10
  53.5 0.0 copy-done.2
  53.5 0.0 copy-done.11
  53.5 0.0 copy-done.12
  53.5 0.0 copy-start.17
  53.5 0.0 copy-start.15
  53.5 0.0 copy-start.16
  53.5 0.0 copy-start.18
  53.5 187.7 %experts.1 = (bf16[8,2,32,2048]{3,2,1,0:T(8,128)(2,1)}, bf16[512,128]{1,0:T(8,128)(2,1)S(1)}, s32[8,128]{1,0:T(8,128)S(1)}) custom-call(bf16[512,2048]{1,0:T(8,128)(2,1)} %bitcast.14, s32[8,512]{1,0:T(8,128)S(1)} %bitcast.18, f32[8,512]{1,0:T(8,128)S(1)} %bitcast.19, bf16[2048,384]{1,0:T(8,128)(2,1)S(1)} %bitcast.15, bf16[2048,384]{1,0:T(8,128)(2,1)} %bitcast.20, ...), custom_call_target="tpu_custom_call" | custom-call | tf_op jit(solution)/shard_map/experts/pallas_call | solution.py:395
  241.3 0.0 copy-start.9
  241.3 0.0 copy-start.13
  241.3 0.6 copy-done.9
  241.9 0.0 copy-done.13
  242.0 0.0 copy-done.17
  242.0 0.0 copy-done.15
  242.0 0.0 copy-start.19
  242.0 0.0 copy-start
  242.0 0.3 copy.27.w_keyval
  242.3 0.0 copy-done.16
  242.3 0.3 convert_reduce_fusion
  242.6 0.0 copy-done.18
  242.6 0.1 add_convert_fusion
  242.7 1.0 fusion
  243.6 0.2 pad_maximum_fusion
  243.9 0.1 concatenate.19
  243.9 0.1 copy.28.segment_column
  244.1 0.0 copy-done.19
  244.1 0.1 copy.29.holders
  244.2 0.0 copy-done
  244.2 0.0 copy-start.3
  244.2 1.2 copy-done.3
  245.4 0.0 copy-start.5
  245.4 1.0 copy-done.5
  246.5 0.0 copy-start.6
  246.5 1.0 copy-done.6
  247.5 0.0 copy-start.14
  247.5 0.7 copy-done.14
  248.2 50.7 %attend.1 = (bf16[512,64]{1,0:T(8,128)(2,1)S(1)}, bf16[512,256]{1,0:T(8,128)(2,1)S(1)}) custom-call(bf16[512,2048]{1,0:T(8,128)(2,1)S(1)} %bitcast.13, bf16[1,2048]{1,0:T(2,128)(2,1)S(1)} %reshape.95.gain, bf16[2048,256]{1,0:T(8,128)(2,1)S(1)} %copy-done.3, bf16[2048,64]{1,0:T(8,128)(2,1)S(1)} %copy.27.w_keyval, f32[512,128]{1,0:T(8,128)S(1)} %get-tuple-element.29.cosine, ...), custom_call_target="tpu_custom_call" | custom-call | tf_op jit(solution)/shard_map/attend/pallas_call | solution.py:621
  298.9 0.0 copy-start.7
  298.9 0.7 copy-done.7
  299.6 0.7 copy.30
  300.3 1.6 copy.33
  301.9 1.7 copy.34
  (7 shorter events, 0.0 us)
Async XLA Ops:
  0.6 52.8 %copy-start.2 = (bf16[1,2048,384]{2,1,0:T(8,128)(2,1)S(1)}, bf16[1,2048,384]{2,1,0:T(8,128)(2,1)}, u32[]{:S(2)}) copy-start(bf16[1,2048,384]{2,1,0:T(8,128)(2,1)} %param.24) | copy-start | bytes 4718596
  1.5 1.2 copy-start.4
  2.7 0.9 copy-start.8
  3.6 0.9 copy-start.10
  4.5 48.9 %copy-start.11 = (s32[512,8]{0,1:T(8,128)S(1)}, s32[512,8]{0,1:T(8,128)}, u32[]{:S(2)}) copy-start(s32[512,8]{0,1:T(8,128)} %param.22) | copy-start | bytes 49156
  4.5 48.9 %copy-start.12 = (f32[512,8]{0,1:T(8,128)S(1)}, f32[512,8]{0,1:T(8,128)}, u32[]{:S(2)}) copy-start(f32[512,8]{0,1:T(8,128)} %param.23) | copy-start | bytes 49156
  51.3 1.3 copy-start.1
  53.5 188.5 %copy-start.17 = (bf16[2048]{0:T(1024)(128)(2,1)S(1)}, bf16[2048]{0:T(1024)(128)(2,1)}, u32[]{:S(2)}) copy-start(bf16[2048]{0:T(1024)(128)(2,1)} %param.21) | copy-start | bytes 12292
  53.5 188.5 %copy-start.15 = (bf16[2048,64]{0,1:T(8,128)(2,1)S(1)}, bf16[2048,64]{0,1:T(8,128)(2,1)}, u32[]{:S(2)}) copy-start(bf16[2048,64]{0,1:T(8,128)(2,1)} %param.28) | copy-start | bytes 786436
  53.5 188.8 %copy-start.16 = (s32[1,504]{1,0:T(1,128)S(1)}, s32[1,504]{1,0:T(1,128)}, u32[]{:S(2)}) copy-start(s32[1,504]{1,0:T(1,128)} %param.29) | copy-start | bytes 6052
  53.5 189.0 %copy-start.18 = (s32[8]{0:T(128)S(1)}, s32[8]{0:T(128)}, u32[]{:S(2)}) copy-start(s32[8]{0:T(128)} %param.30) | copy-start | bytes 100
  241.3 0.7 copy-start.9
  241.3 0.6 copy-start.13
  242.0 2.1 copy-start.19
  242.0 2.2 copy-start
  244.2 1.2 copy-start.3
  245.4 1.0 copy-start.5
  246.5 1.0 copy-start.6
  247.5 0.7 copy-start.14
  298.9 0.7 copy-start.7

commit v3 on v2

--- a/solution.py
+++ b/solution.py
@@ -202,6 +202,13 @@
     return value.reshape(8, 2, BLOCK, value.shape[-1])
 
 
+def fetch(pairs, sems):
+    copies = [pltpu.make_async_copy(far, near, sems.at[index]) for index, (far, near) in enumerate(pairs)]
+    for copy in copies:
+        copy.start()
+    return copies
+
+
 def out_kernel(context, w_out, residual, gain, normed, mid, blocks, *rest):
     buffers, (send, recv) = rest[:6], rest[6:]
     place = around()
@@ -258,15 +265,33 @@
     )(context, w_out, residual, gain.reshape(1, D))
 
 
-GROUPS = (8, 12, 4, 0)
-TABLE_SEMS = 32 + 2 * RING_SEMS
+SPLIT = (4, 5, 10, 11, 12, 13, 14, 15)
+SENDS = (12, 14, 2, 10, 4, 6, 8, 0)
+PLAN = (
+    ('pass', (12, 13, 14, 15)),
+    ('work', (0,)),
+    ('pass', (10, 11)),
+    ('work', (12,)),
+    ('pass', (4, 5)),
+    ('work', (8,)),
+    ('give', (12, 13, 14, 15)),
+    ('work', (4,)),
+    ('give', (10, 11, 4, 5)),
+)
+WHOLE_RUNS = ((0, 4), (6, 10))
+SPLIT_RUNS = ((10, 12), (12, 16), (4, 6))
+SHARE_SEMS = 32
+SWAP_SEMS = 48
+RING_BASE = 64
+TABLE_SEMS = RING_BASE + 2 * RING_SEMS
 
 
 def expert_kernel(
-    normed, routes, scores, w_gate, w_up, w_down, mid, table, full, share, tables,
+    normed, routes, scores, far_gate, far_up, far_down, mid, table, full, share, tables,
     blocks, y_left, up_left, down_left, up_right, down_right, y_right,
-    going, coming, back, total, weights, listed, send, recv,
+    going, coming, result, back, swapped, total, weights, listed, w_gate, w_up, w_down, fetched, send, recv,
 ):
+    fetches = fetch(((far_gate, w_gate), (far_up, w_up), (far_down, w_down)), fetched)
     row = lax.axis_index("row")
     place = around()
     z, y, after, before, beside = place
@@ -302,41 +327,68 @@
     )
     rank = jnp.where(hit > 0.0, rank, -1.0).astype(jnp.int32)
     slots = lax.broadcasted_iota(jnp.int32, (CAP, ROWS), 0)
-    pl.semaphore_wait(barrier, 18)
+    mine = y * HALF_D
+    theirs = HALF_D - mine
+
+    def half(start):
+        return pl.ds(pl.multiple_of(start, HALF_D), HALF_D)
+
+    def piece(start, tile):
+        return pl.ds(pl.multiple_of(start + tile, TILE), TILE)
+
     started = []
-    arrivals = {}
-    lists = []
-    for o in range(1, 16):
-        copy = remote(table, listed.at[o], send, recv, TABLE_SEMS + o, partner(o, 1))
+
+    def go(src, dst, index, device):
+        copy = remote(src, dst, send, recv, index, device)
         copy.start()
-        lists.append(copy)
-    for group in GROUPS:
+        started.append(copy)
+        return copy
+
+    def choose(chunks):
         picks = []
-        for o in range(group, group + 4):
+        for o in chunks:
             chosen = slots == rank[o : o + 1, :]
             picks.append(jnp.where(chosen, 1.0, 0.0).astype(jnp.bfloat16))
             weights[o * CAP : (o + 1) * CAP, :] = jnp.where(chosen, weight[o : o + 1, :], 0.0).astype(
                 jnp.bfloat16
             )
-        pick = jnp.concatenate(picks, axis=0)
-        for tile in range(0, D, TILE):
-            columns = pl.ds(tile, TILE)
+        return jnp.concatenate(picks, axis=0)
+
+    arrivals = {}
+    for low in SENDS:
+        pick = choose((low, low + 1))
+        for tile in range(0, HALF_D if low in SPLIT else D, TILE):
+            columns = piece(mine, tile) if low in SPLIT else pl.ds(tile, TILE)
             value = jnp.dot(pick, normed[:, columns], preferred_element_type=jnp.float32)
-            value = value.astype(jnp.bfloat16).reshape(4, CAP, TILE)
-            if group:
-                going[group : group + 4, :, columns] = value
+            value = value.astype(jnp.bfloat16).reshape(2, CAP, TILE)
+            if low:
+                going[low : low + 2, :, columns] = value
             else:
                 coming[0, :, columns] = value[0]
-                going[1:4, :, columns] = value[1:]
-        for o in range(max(group, 1), group + 4):
-            copy = remote(going.at[o], coming.at[o], send, recv, o, partner(o, 1))
-            copy.start()
-            started.append(copy)
-            arrivals[o] = copy
-    returns = {}
-    for group in GROUPS:
-        for o in range(max(group, 1), group + 4):
-            arrivals[o].wait_recv()
+                going[1, :, columns] = value[1]
+        if low == SENDS[0]:
+            pl.semaphore_wait(barrier, 18)
+        for o in (low, low + 1):
+            if o in SPLIT:
+                arrivals[o] = go(going.at[o, :, half(mine)], coming.at[o, :, half(mine)], o, partner(o, 1))
+            elif o:
+                arrivals[o] = go(going.at[o], coming.at[o], o, partner(o, 1))
+    lists = [go(table, listed.at[o], TABLE_SEMS + o, partner(o, 1)) for o in range(1, 16)]
+    shared = {}
+
+    def pass_on(o):
+        columns = half(theirs if o >= 8 else mine)
+        arrivals[o].wait_recv()
+        shared[o] = go(coming.at[o, :, columns], coming.at[o, :, columns], SHARE_SEMS + o, beside)
+
+    returns, swaps = {}, {}
+
+    def work(group):
+        for o in range(group, group + 4):
+            if o in SPLIT:
+                shared[o].wait_recv()
+            elif o:
+                arrivals[o].wait_recv()
         rows = coming[group : group + 4].reshape(4 * CAP, D)
         gate = jnp.dot(rows, w_gate[...], preferred_element_type=jnp.float32)
         up = jnp.dot(rows, w_up[...], preferred_element_type=jnp.float32)
@@ -344,45 +396,76 @@
         for tile in range(0, D, TILE):
             columns = pl.ds(tile, TILE)
             value = jnp.dot(inner, w_down[:, columns], preferred_element_type=jnp.float32)
-            coming[group : group + 4, :, columns] = value.astype(jnp.bfloat16).reshape(4, CAP, TILE)
-        for o in range(max(group, 1), group + 4):
-            copy = remote(coming.at[o], back.at[o], send, recv, 16 + o, partner(o, -1))
-            copy.start()
-            started.append(copy)
-            returns[o] = copy
-    back[0] = coming[0]
+            result[group : group + 4, :, columns] = value.astype(jnp.bfloat16).reshape(4, CAP, TILE)
+        for o in range(group, group + 4):
+            if o in SPLIT:
+                columns = half(mine if o >= 8 else theirs)
+                swaps[o] = go(result.at[o, :, columns], swapped.at[o], SWAP_SEMS + o, beside)
+            elif o:
+                returns[o] = go(result.at[o], back.at[o], 16 + o, partner(o, -1))
+
+    def give(o):
+        columns = half(theirs if o >= 8 else mine)
+        swaps[o].wait_recv()
+        result[o, :, columns] = (
+            result[o, :, columns].astype(jnp.float32) + swapped[o].astype(jnp.float32)
+        ).astype(jnp.bfloat16)
+        returns[o] = go(result.at[o, :, columns], back.at[o, :, columns], 16 + o, partner(o, -1))
+
+    for copy in fetches:
+        copy.wait()
+    for task, chunks in PLAN:
+        for o in chunks:
+            {"pass": pass_on, "work": work, "give": give}[task](o)
+    back[0] = result[0]
     for copy in lists:
         copy.wait_recv()
     known = table[...]
     for o in range(1, 16):
         known = known + listed[o]
     tables[...] = known
-    for index, group in enumerate(GROUPS[::-1]):
-        for o in range(max(group, 1), group + 4):
+
+    def combine(low, high, columns):
+        count = (high - low) * CAP
+        return lax.dot_general(
+            weights[low * CAP : high * CAP, :],
+            back[low:high, :, columns].reshape(count, TILE),
+            (((0,), (0,)), ((), ())),
+            preferred_element_type=jnp.float32,
+        )
+
+    for low, high in WHOLE_RUNS:
+        for o in range(max(low, 1), high):
             returns[o].wait_recv()
-        spread = weights[group * CAP : (group + 4) * CAP, :]
         for tile in range(0, D, TILE):
             columns = pl.ds(tile, TILE)
-            value = lax.dot_general(
-                spread,
-                back[group : group + 4, :, columns].reshape(4 * CAP, TILE),
-                (((0,), (0,)), ((), ())),
-                preferred_element_type=jnp.float32,
-            )
-            if index:
-                value = value + total[:, columns]
-            if index < 3:
+            value = combine(low, high, columns)
+            total[:, columns] = value if low == 0 else total[:, columns] + value
+
+    def settle(columns, value):
+        value = by_block(value.astype(jnp.bfloat16))
+        blocks[0, :, :, columns] = value[:, 0]
+        blocks[1, :, :, columns] = value[:, 1]
+
+    for tile in range(0, HALF_D, TILE):
+        columns = piece(theirs, tile)
+        settle(columns, total[:, columns])
+    for low, high in SPLIT_RUNS:
+        for o in range(low, high):
+            returns[o].wait_recv()
+        for tile in range(0, HALF_D, TILE):
+            columns = piece(mine, tile)
+            value = total[:, columns] + combine(low, high, columns)
+            if (low, high) == SPLIT_RUNS[-1]:
+                settle(columns, value)
+            else:
                 total[:, columns] = value
-            else:
-                value = by_block(value.astype(jnp.bfloat16))
-                blocks[0, :, :, columns] = value[:, 0]
-                blocks[1, :, :, columns] = value[:, 1]
     left, right, ring = reduce_blocks(
-        place, blocks, y_left, up_left, down_left, up_right, down_right, y_right, send, recv, 32
+        place, blocks, y_left, up_left, down_left, up_right, down_right, y_right, send, recv, RING_BASE
     )
     full[z, y, :, LEFT] = (mid[:, :HALF_D].astype(jnp.float32) + left).astype(jnp.bfloat16)
     full[z, y, :, RIGHT] = (mid[:, HALF_D:].astype(jnp.float32) + right).astype(jnp.bfloat16)
-    started = started + lists + ring + gather_blocks(place, full, send, recv, 32 + RING_SEMS)
+    started = started + ring + gather_blocks(place, full, send, recv, RING_BASE + RING_SEMS)
     own = pl.ds(pl.multiple_of((z * 2 + y) * 128, 128), 128)
     share[...] = full[:, :, :, own].reshape(ROWS, 128)
     for copy in started:
@@ -399,21 +482,27 @@
             jax.ShapeDtypeStruct((ROWS, 128), jnp.bfloat16),
             jax.ShapeDtypeStruct((8, 128), jnp.int32),
         ),
-        in_specs=[vmem] * 8,
+        in_specs=[vmem] * 3 + [pl.BlockSpec(memory_space=pltpu.HBM)] * 3 + [vmem] * 2,
         out_specs=(vmem, vmem, vmem),
         scratch_shapes=ring_scratch()
         + [
             pltpu.VMEM((16, CAP, D), jnp.bfloat16),
             pltpu.VMEM((16, CAP, D), jnp.bfloat16),
             pltpu.VMEM((16, CAP, D), jnp.bfloat16),
+            pltpu.VMEM((16, CAP, D), jnp.bfloat16),
+            pltpu.VMEM((16, CAP, HALF_D), jnp.bfloat16),
             pltpu.VMEM((ROWS, D), jnp.float32),
             pltpu.VMEM((16 * CAP, ROWS), jnp.bfloat16),
             pltpu.VMEM((16, 8, 128), jnp.int32),
+            pltpu.VMEM((D, 384), jnp.bfloat16),
+            pltpu.VMEM((D, 384), jnp.bfloat16),
+            pltpu.VMEM((384, D), jnp.bfloat16),
+            pltpu.SemaphoreType.DMA((3,)),
             pltpu.SemaphoreType.DMA((sems,)),
             pltpu.SemaphoreType.DMA((sems,)),
         ],
         compiler_params=pltpu.CompilerParams(
-            collective_id=1, has_side_effects=True, vmem_limit_bytes=52 << 20
+            collective_id=1, has_side_effects=True, vmem_limit_bytes=56 << 20
         ),
         name="experts",
     )(normed, routes, scores, w_gate, w_up, w_down, mid, table)
@@ -434,11 +523,22 @@
 
 
 def attend_kernel(
-    full, gain, w_query, w_keyval, cosine, sine, segment_column, segment_row, holders, tables,
-    cache_keys, cache_values, new_cache, attention,
+    full, gain, far_query, far_keyval, far_cosine, far_sine, segment_column, segment_row, holders, tables,
+    far_keys, far_values, new_cache, attention,
     x_in, query, pieces, keys, values, own_query, all_query, slot_query, slots_query,
-    parts, parts_in, reply, replies, send, recv,
+    parts, parts_in, reply, replies, w_query, w_keyval, cosine, sine, cache_keys, cache_values, fetched, send, recv,
 ):
+    fetches = fetch(
+        (
+            (far_query, w_query),
+            (far_cosine, cosine),
+            (far_sine, sine),
+            (far_keyval, w_keyval),
+            (far_keys, cache_keys),
+            (far_values, cache_values),
+        ),
+        fetched,
+    )
     row = lax.axis_index("row")
     col = lax.axis_index("col")
     quarter = lax.rem(col, 4)
@@ -466,6 +566,8 @@
         inverse = lax.rsqrt(jnp.mean(value * value, axis=-1, keepdims=True) + EPSILON)
         return (value * inverse * gains).astype(jnp.bfloat16)
 
+    for copy in fetches[:3]:
+        copy.wait()
     early = jnp.dot(norm(full[:16, :]), w_query[...], preferred_element_type=jnp.float32)
     early = early.astype(jnp.bfloat16).astype(jnp.float32)
     for head in range(2):
@@ -477,6 +579,8 @@
     asks = [go(own_query, all_query.at[row], o, along_row(o)) for o in range(1, 16)]
     for tile in range(0, ROWS, 64):
         x_in[tile : tile + 64, :] = norm(full[tile : tile + 64, :])
+    for copy in fetches[3:]:
+        copy.wait()
     keyval = jnp.dot(x_in[...], w_keyval[...], preferred_element_type=jnp.float32).astype(jnp.bfloat16)
     pieces[quarter] = jnp.concatenate([keyval[: ROWS // 2], keyval[ROWS // 2 :]], axis=1)
     shares = [
@@ -617,6 +721,7 @@
 
 def attend(full, gain, w_query, w_keyval, cosine, sine, segments, holders, tables, cache_keys, cache_values):
     vmem = pl.BlockSpec(memory_space=pltpu.VMEM)
+    far = pl.BlockSpec(memory_space=pltpu.HBM)
     f32, bf16 = jnp.float32, jnp.bfloat16
     return pl.pallas_call(
         attend_kernel,
@@ -624,7 +729,7 @@
             jax.ShapeDtypeStruct((ROWS, 64), bf16),
             jax.ShapeDtypeStruct((ROWS, 2 * HD), bf16),
         ),
-        in_specs=[vmem] * 12,
+        in_specs=[vmem] * 2 + [far] * 4 + [vmem] * 4 + [far] * 2,
         out_specs=(vmem, vmem),
         scratch_shapes=[
             pltpu.VMEM((ROWS, D), bf16),
@@ -640,6 +745,13 @@
             pltpu.VMEM((16, 8, PACK), f32),
             pltpu.VMEM((8, PACK), f32),
             pltpu.VMEM((16, 8, PACK), f32),
+            pltpu.VMEM((D, 2 * HD), bf16),
+            pltpu.VMEM((D, 64), bf16),
+            pltpu.VMEM((ROWS, HD), f32),
+            pltpu.VMEM((ROWS, HD), f32),
+            pltpu.VMEM((8, 64, 4 * HD), bf16),
+            pltpu.VMEM((8, 64, 4 * HD), bf16),
+            pltpu.SemaphoreType.DMA((6,)),
             pltpu.SemaphoreType.DMA((68,)),
             pltpu.SemaphoreType.DMA((68,)),
         ],

time: 304 us -> 236 us (0.78)
  Pallas kernels: 285 us -> 217 us
    pallas_call x1, Pallas kernels: 188 us -> 132 us  [experts(): pl.pallas_call(expert_kernel, out_shape=(jax.ShapeDtypeStruct((8, 2, BLOC...]
    pallas_call x1, Pallas kernels: 50.7 us -> 38.2 us  [attend(): pl.pallas_call(attend_kernel, out_shape=(jax.ShapeDtypeStruct((ROWS, 64),...]
    unnamed x44 -> x36, local copies, waits for them, and re-layouts: 14 us -> 14 us
where the time goes in v3:
time: 236 us
  Pallas kernels  217 us (92%)
  local copies, waits for them, and re-layouts  15.1 us (6%)
  other arithmetic  2.82 us (1%)
    pallas_call x1, Pallas kernels, experts(): pl.pallas_call(expert_kernel, out_shape=(jax.ShapeDtypeStruct((8, 2, BLOC...  132 us
    pallas_call x1, Pallas kernels, out_project(): pl.pallas_call(out_kernel, out_shape=(jax.ShapeDtypeStruct((8, 2, BLOCK,...  46.8 us
    pallas_call x1, Pallas kernels, attend(): pl.pallas_call(attend_kernel, out_shape=(jax.ShapeDtypeStruct((ROWS, 64),...  38.2 us
    unnamed x36, local copies, waits for them, and re-layouts  14 us

profile of v3, /device:TPU:1, one launch (start us, length us, event | category | flops | bytes accessed | tf_op | source)
XLA Modules:
  0.0 235.7 jit_solution(6414295895538954672)
XLA Ops:
  0.6 0.7 reshape.92.gain
  1.3 0.0 copy-start.3
  1.3 1.2 copy-done.3
  2.5 0.0 copy-start.7
  2.6 0.9 copy-done.7
  3.5 0.0 copy-start.9
  3.5 0.9 copy-done.9
  4.4 46.8 %out_project.1 = (bf16[8,2,32,2048]{3,2,1,0:T(8,128)(2,1)S(1)}, bf16[32,2048]{1,0:T(8,128)(2,1)S(1)}) custom-call(bf16[512,256]{1,0:T(8,128)(2,1)S(1)} %copy-done.7, bf16[256,2048]{1,0:T(8,128)(2,1)S(1)} %copy-done.3, bf16[512,128]{1,0:T(8,128)(2,1)S(1)} %copy-done.9, bf16[1,2048]{1,0:T(2,128)(2,1)S(1)} %reshape.92.gain), custom_call_target="tpu_custom_call" | custom-call | tf_op jit(solution)/shard_map/out_project/pallas_call | solution.py:251
  51.2 0.0 copy-start.1
  51.2 1.3 copy-done.1
  52.6 0.0 copy-start.8
  52.6 0.7 copy-done.8
  53.2 0.7 pad_add_fusion
  53.9 0.1 tile.10
  54.0 0.6 broadcast_select_fusion.table
  54.6 0.0 copy-start.13
  54.6 0.0 copy-start.11
  54.6 0.0 copy-start.12
  54.6 0.0 copy-start.14
  54.6 132.0 %experts.1 = (bf16[8,2,32,2048]{3,2,1,0:T(8,128)(2,1)}, bf16[512,128]{1,0:T(8,128)(2,1)}, s32[8,128]{1,0:T(8,128)}) custom-call(bf16[512,2048]{1,0:T(8,128)(2,1)} %bitcast.14, s32[8,512]{1,0:T(8,128)} %bitcast.22, f32[8,512]{1,0:T(8,128)} %bitcast.23, bf16[2048,384]{1,0:T(8,128)(2,1)} %bitcast.17, bf16[2048,384]{1,0:T(8,128)(2,1)} %bitcast.18, ...), custom_call_target="tpu_custom_call" | custom-call | tf_op jit(solution)/shard_map/experts/pallas_call | solution.py:478
  186.6 0.0 copy-done.13
  186.6 0.0 copy-done.11
  186.6 0.0 copy-start.15
  186.6 0.0 copy-start
  186.7 0.3 copy.27.far_keyval
  186.9 0.0 copy-done.12
  187.0 0.3 convert_reduce_fusion
  187.2 0.0 copy-done.14
  187.2 0.1 add_convert_fusion
  187.3 1.0 fusion
  188.3 0.2 pad_maximum_fusion
  188.5 0.1 concatenate.19
  188.6 0.1 copy.28.segment_column
  188.7 0.0 copy-done.15
  188.8 0.1 copy.29.holders
  188.8 0.0 copy-done
  188.8 0.0 copy-start.2
  188.8 1.2 copy-done.2
  190.1 0.0 copy-start.4
  190.1 1.0 copy-done.4
  191.1 0.0 copy-start.5
  191.1 1.0 copy-done.5
  192.2 0.0 copy-start.10
  192.2 0.7 copy-done.10
  192.8 38.2 %attend.1 = (bf16[512,64]{1,0:T(8,128)(2,1)S(1)}, bf16[512,256]{1,0:T(8,128)(2,1)S(1)}) custom-call(bf16[512,2048]{1,0:T(8,128)(2,1)S(1)} %bitcast.13, bf16[1,2048]{1,0:T(2,128)(2,1)S(1)} %reshape.95.gain, bf16[2048,256]{1,0:T(8,128)(2,1)S(1)} %copy-done.2, bf16[2048,64]{1,0:T(8,128)(2,1)S(1)} %copy.27.far_keyval, ...), custom_call_target="tpu_custom_call" | custom-call | tf_op jit(solution)/shard_map/attend/pallas_call | solution.py:726
  231.0 0.0 copy-start.6
  231.0 0.7 copy-done.6
  231.7 0.7 copy.30
  232.4 1.6 copy.33
  234.0 1.7 copy.34
  (6 shorter events, 0.0 us)
Async XLA Ops:
  1.3 1.2 copy-start.3
  2.5 0.9 copy-start.7
  3.5 0.9 copy-start.9
  51.2 1.3 copy-start.1
  52.6 0.7 copy-start.8
  54.6 132.0 %copy-start.13 = (bf16[2048]{0:T(1024)(128)(2,1)S(1)}, bf16[2048]{0:T(1024)(128)(2,1)}, u32[]{:S(2)}) copy-start(bf16[2048]{0:T(1024)(128)(2,1)} %param.21) | copy-start | bytes 12292
  54.6 132.0 %copy-start.11 = (bf16[2048,64]{0,1:T(8,128)(2,1)S(1)}, bf16[2048,64]{0,1:T(8,128)(2,1)}, u32[]{:S(2)}) copy-start(bf16[2048,64]{0,1:T(8,128)(2,1)} %param.28) | copy-start | bytes 786436
  54.6 132.3 %copy-start.12 = (s32[1,504]{1,0:T(1,128)S(1)}, s32[1,504]{1,0:T(1,128)}, u32[]{:S(2)}) copy-start(s32[1,504]{1,0:T(1,128)} %param.29) | copy-start | bytes 6052
  54.6 132.6 %copy-start.14 = (s32[8]{0:T(128)S(1)}, s32[8]{0:T(128)}, u32[]{:S(2)}) copy-start(s32[8]{0:T(128)} %param.30) | copy-start | bytes 100
  186.6 2.1 copy-start.15
  186.6 2.2 copy-start
  188.8 1.2 copy-start.2
  190.1 1.0 copy-start.4
  191.1 1.0 copy-start.5
  192.2 0.7 copy-start.10
  231.0 0.7 copy-start.6

commit v4 on v3

--- a/solution.py
+++ b/solution.py
@@ -209,11 +209,9 @@
     return copies
 
 
-def out_kernel(context, w_out, residual, gain, normed, mid, blocks, *rest):
-    buffers, (send, recv) = rest[:6], rest[6:]
+def project(context, w_out, residual, gain, normed, mid, blocks, buffers, send, recv, wait_for_all):
     place = around()
-    z, y, after, before, beside = place
-    barrier = greet((after, before, beside))
+    z, y = place[:2]
     for tile in range(0, D, TILE):
         columns = pl.ds(tile, TILE)
         value = by_block(
@@ -226,7 +224,7 @@
     value = by_block((value + residual[...].astype(jnp.float32)).astype(jnp.bfloat16))
     blocks[0, :, :, own] = value[:, 0]
     blocks[1, :, :, own] = value[:, 1]
-    pl.semaphore_wait(barrier, 3)
+    wait_for_all()
     left, right, started = reduce_blocks(place, blocks, *buffers, send, recv, 0)
     left = left.astype(jnp.bfloat16)
     right = right.astype(jnp.bfloat16)
@@ -241,28 +239,7 @@
     gains = gain[...].astype(jnp.float32)
     normed[z, y, :, LEFT] = (left * inverse * gains[:, :HALF_D]).astype(jnp.bfloat16)
     normed[z, y, :, RIGHT] = (right * inverse * gains[:, HALF_D:]).astype(jnp.bfloat16)
-    started = started + gather_blocks(place, normed, send, recv, RING_SEMS)
-    for copy in started:
-        copy.wait_send()
-
-
-def out_project(context, w_out, residual, gain):
-    vmem = pl.BlockSpec(memory_space=pltpu.VMEM)
-    return pl.pallas_call(
-        out_kernel,
-        out_shape=(
-            jax.ShapeDtypeStruct((8, 2, BLOCK, D), jnp.bfloat16),
-            jax.ShapeDtypeStruct((BLOCK, D), jnp.bfloat16),
-        ),
-        in_specs=[vmem] * 4,
-        out_specs=(vmem, vmem),
-        scratch_shapes=ring_scratch()
-        + [pltpu.SemaphoreType.DMA((2 * RING_SEMS,)), pltpu.SemaphoreType.DMA((2 * RING_SEMS,))],
-        compiler_params=pltpu.CompilerParams(
-            collective_id=0, has_side_effects=True, vmem_limit_bytes=40 << 20
-        ),
-        name="out_project",
-    )(context, w_out, residual, gain.reshape(1, D))
+    return started + gather_blocks(place, normed, send, recv, RING_SEMS)
 
 
 SPLIT = (4, 5, 10, 11, 12, 13, 14, 15)
@@ -286,24 +263,25 @@
 TABLE_SEMS = RING_BASE + 2 * RING_SEMS
 
 
-def expert_kernel(
-    normed, routes, scores, far_gate, far_up, far_down, mid, table, full, share, tables,
-    blocks, y_left, up_left, down_left, up_right, down_right, y_right,
-    going, coming, result, back, swapped, total, weights, listed, w_gate, w_up, w_down, fetched, send, recv,
+def partner(o, sign):
+    row = lax.axis_index("row")
+    col = lax.axis_index("col")
+    z, y = col // 2, lax.rem(col, 2)
+    yh, x, core = row // 8, lax.rem(row // 2, 4), lax.rem(row, 2)
+    a, b, d = o // 8, (o // 2) % 4, o % 2
+    there = lax.rem(yh + a, 2) * 8 + lax.rem(x + sign * b + 4, 4) * 2 + lax.rem(core + d, 2)
+    return (there, z * 2 + lax.rem(y + a, 2))
+
+
+def apply_experts(
+    normed, routes, scores, w_gate, w_up, w_down, fetches, mid, table, full, share, tables,
+    blocks, buffers, going, coming, result, back, swapped, total, weights, listed, send, recv,
 ):
-    fetches = fetch(((far_gate, w_gate), (far_up, w_up), (far_down, w_down)), fetched)
     row = lax.axis_index("row")
     place = around()
     z, y, after, before, beside = place
     yh, x, core = row // 8, lax.rem(row // 2, 4), lax.rem(row, 2)
 
-    def partner(o, sign):
-        a, b, d = o // 8, (o // 2) % 4, o % 2
-        there = lax.rem(yh + a, 2) * 8 + lax.rem(x + sign * b + 4, 4) * 2 + lax.rem(core + d, 2)
-        return (there, z * 2 + lax.rem(y + a, 2))
-
-    partners = [partner(o, 1) for o in range(1, 16)]
-    barrier = greet([after, before, beside] + partners)
     offsets = lax.broadcasted_iota(jnp.int32, (16, 1), 0)
     a, b, d = offsets // 8, lax.rem(offsets // 2, 4), lax.rem(offsets, 2)
     expert = (
@@ -359,15 +337,14 @@
         pick = choose((low, low + 1))
         for tile in range(0, HALF_D if low in SPLIT else D, TILE):
             columns = piece(mine, tile) if low in SPLIT else pl.ds(tile, TILE)
-            value = jnp.dot(pick, normed[:, columns], preferred_element_type=jnp.float32)
+            rows = normed[:, :, :, columns].reshape(ROWS, TILE)
+            value = jnp.dot(pick, rows, preferred_element_type=jnp.float32)
             value = value.astype(jnp.bfloat16).reshape(2, CAP, TILE)
             if low:
                 going[low : low + 2, :, columns] = value
             else:
                 coming[0, :, columns] = value[0]
                 going[1, :, columns] = value[1]
-        if low == SENDS[0]:
-            pl.semaphore_wait(barrier, 18)
         for o in (low, low + 1):
             if o in SPLIT:
                 arrivals[o] = go(going.at[o, :, half(mine)], coming.at[o, :, half(mine)], o, partner(o, 1))
@@ -461,51 +438,14 @@
             else:
                 total[:, columns] = value
     left, right, ring = reduce_blocks(
-        place, blocks, y_left, up_left, down_left, up_right, down_right, y_right, send, recv, RING_BASE
+        place, blocks, *buffers, send, recv, RING_BASE
     )
     full[z, y, :, LEFT] = (mid[:, :HALF_D].astype(jnp.float32) + left).astype(jnp.bfloat16)
     full[z, y, :, RIGHT] = (mid[:, HALF_D:].astype(jnp.float32) + right).astype(jnp.bfloat16)
     started = started + ring + gather_blocks(place, full, send, recv, RING_BASE + RING_SEMS)
     own = pl.ds(pl.multiple_of((z * 2 + y) * 128, 128), 128)
     share[...] = full[:, :, :, own].reshape(ROWS, 128)
-    for copy in started:
-        copy.wait_send()
-
-
-def experts(normed, routes, scores, w_gate, w_up, w_down, mid, table):
-    vmem = pl.BlockSpec(memory_space=pltpu.VMEM)
-    sems = TABLE_SEMS + 16
-    return pl.pallas_call(
-        expert_kernel,
-        out_shape=(
-            jax.ShapeDtypeStruct((8, 2, BLOCK, D), jnp.bfloat16),
-            jax.ShapeDtypeStruct((ROWS, 128), jnp.bfloat16),
-            jax.ShapeDtypeStruct((8, 128), jnp.int32),
-        ),
-        in_specs=[vmem] * 3 + [pl.BlockSpec(memory_space=pltpu.HBM)] * 3 + [vmem] * 2,
-        out_specs=(vmem, vmem, vmem),
-        scratch_shapes=ring_scratch()
-        + [
-            pltpu.VMEM((16, CAP, D), jnp.bfloat16),
-            pltpu.VMEM((16, CAP, D), jnp.bfloat16),
-            pltpu.VMEM((16, CAP, D), jnp.bfloat16),
-            pltpu.VMEM((16, CAP, D), jnp.bfloat16),
-            pltpu.VMEM((16, CAP, HALF_D), jnp.bfloat16),
-            pltpu.VMEM((ROWS, D), jnp.float32),
-            pltpu.VMEM((16 * CAP, ROWS), jnp.bfloat16),
-            pltpu.VMEM((16, 8, 128), jnp.int32),
-            pltpu.VMEM((D, 384), jnp.bfloat16),
-            pltpu.VMEM((D, 384), jnp.bfloat16),
-            pltpu.VMEM((384, D), jnp.bfloat16),
-            pltpu.SemaphoreType.DMA((3,)),
-            pltpu.SemaphoreType.DMA((sems,)),
-            pltpu.SemaphoreType.DMA((sems,)),
-        ],
-        compiler_params=pltpu.CompilerParams(
-            collective_id=1, has_side_effects=True, vmem_limit_bytes=56 << 20
-        ),
-        name="experts",
-    )(normed, routes, scores, w_gate, w_up, w_down, mid, table)
+    return started
 
 
 SCALE = HD ** (-0.5)
@@ -522,35 +462,25 @@
     )
 
 
-def attend_kernel(
-    full, gain, far_query, far_keyval, far_cosine, far_sine, segment_column, segment_row, holders, tables,
-    far_keys, far_values, new_cache, attention,
+def along_row(o):
+    return (lax.rem(lax.axis_index("row") + o, 16), lax.axis_index("col"))
+
+
+def along_col(o):
+    return (lax.axis_index("row"), lax.rem(lax.axis_index("col") + o, 16))
+
+
+def attend(
+    full, gain, w_query, w_keyval, cosine, sine, fetches, segment_column, segment_row, holders, tables,
+    cache_keys, cache_values, new_cache, attention,
     x_in, query, pieces, keys, values, own_query, all_query, slot_query, slots_query,
-    parts, parts_in, reply, replies, w_query, w_keyval, cosine, sine, cache_keys, cache_values, fetched, send, recv,
+    parts, parts_in, reply, replies, send, recv,
 ):
-    fetches = fetch(
-        (
-            (far_query, w_query),
-            (far_cosine, cosine),
-            (far_sine, sine),
-            (far_keyval, w_keyval),
-            (far_keys, cache_keys),
-            (far_values, cache_values),
-        ),
-        fetched,
-    )
     row = lax.axis_index("row")
     col = lax.axis_index("col")
     quarter = lax.rem(col, 4)
     first = col - quarter
 
-    def along_row(o):
-        return (lax.rem(row + o, 16), col)
-
-    def along_col(o):
-        return (row, lax.rem(col + o, 16))
-
-    barrier = greet([along_row(o) for o in range(1, 16)] + [along_col(o) for o in range(1, 16)])
     started = []
 
     def go(src, dst, index, device):
@@ -566,21 +496,18 @@
         inverse = lax.rsqrt(jnp.mean(value * value, axis=-1, keepdims=True) + EPSILON)
         return (value * inverse * gains).astype(jnp.bfloat16)
 
-    for copy in fetches[:3]:
+    for copy in fetches:
         copy.wait()
-    early = jnp.dot(norm(full[:16, :]), w_query[...], preferred_element_type=jnp.float32)
+    early = jnp.dot(norm(full[0, 0, :16, :]), w_query[...], preferred_element_type=jnp.float32)
     early = early.astype(jnp.bfloat16).astype(jnp.float32)
     for head in range(2):
         span = pl.ds(head * HD, HD)
         turned = turn(early[:, head * HD : (head + 1) * HD], cosine[:16, :], sine[:16, :])
         own_query[:, span] = turned.astype(jnp.bfloat16).astype(jnp.float32)[:8]
     all_query[row] = own_query[...]
-    pl.semaphore_wait(barrier, 30)
     asks = [go(own_query, all_query.at[row], o, along_row(o)) for o in range(1, 16)]
     for tile in range(0, ROWS, 64):
-        x_in[tile : tile + 64, :] = norm(full[tile : tile + 64, :])
-    for copy in fetches[3:]:
-        copy.wait()
+        x_in[tile : tile + 64, :] = norm(full[tile // 64].reshape(64, D))
     keyval = jnp.dot(x_in[...], w_keyval[...], preferred_element_type=jnp.float32).astype(jnp.bfloat16)
     pieces[quarter] = jnp.concatenate([keyval[: ROWS // 2], keyval[ROWS // 2 :]], axis=1)
     shares = [
@@ -715,23 +642,88 @@
         attention[:16, span] = jnp.where(
             decoded, result, attention[:16, span].astype(jnp.float32)
         ).astype(jnp.bfloat16)
+    return started
+
+
+def layer_kernel(
+    far_context, far_out, far_residual, gain_post, routes, scores, far_gate, far_up, far_down, table,
+    gain_input, far_query, far_keyval, far_cosine, far_sine, segment_column, segment_row, holders,
+    far_keys, far_values, share, new_cache, attention, context, w_out, residual, w_gate, w_up, w_down,
+    w_query, w_keyval, cosine, sine, cache_keys, cache_values, normed, full, mid, tables, *rest,
+):
+    first_ring, second_ring, rest = rest[:7], rest[7:14], rest[14:]
+    exchange, rest = rest[:8], rest[8:]
+    heads, (fetched, *sems) = rest[:13], rest[13:]
+    near = (context, w_out, residual, w_gate, w_up, w_down)
+    near = near + (w_query, w_keyval, cosine, sine, cache_keys, cache_values)
+    far = (far_context, far_out, far_residual, far_gate, far_up, far_down)
+    far = far + (far_query, far_keyval, far_cosine, far_sine, far_keys, far_values)
+    fetches = fetch(zip(far, near), fetched)
+    peers = [along_row(o) for o in range(1, 16)] + [along_col(o) for o in range(1, 16)]
+    peers = peers + [partner(o, 1) for o in range(8, 16)]
+    barrier = greet(peers)
+    for copy in fetches[:3]:
+        copy.wait()
+    started = project(
+        context, w_out, residual, gain_post, normed, mid, first_ring[0], first_ring[1:], *sems[:2],
+        lambda: pl.semaphore_wait(barrier, len(peers)),
+    )
+    started = started + apply_experts(
+        normed, routes, scores, w_gate, w_up, w_down, fetches[3:6], mid, table, full, share, tables,
+        second_ring[0], second_ring[1:], *exchange, *sems[2:4],
+    )
+    started = started + attend(
+        full, gain_input, w_query, w_keyval, cosine, sine, fetches[6:], segment_column, segment_row,
+        holders, tables, cache_keys, cache_values, new_cache, attention, *heads, *sems[4:],
+    )
     for copy in started:
         copy.wait_send()
 
 
-def attend(full, gain, w_query, w_keyval, cosine, sine, segments, holders, tables, cache_keys, cache_values):
+def layer(*operands):
     vmem = pl.BlockSpec(memory_space=pltpu.VMEM)
     far = pl.BlockSpec(memory_space=pltpu.HBM)
-    f32, bf16 = jnp.float32, jnp.bfloat16
+    f32, bf16, i32 = jnp.float32, jnp.bfloat16, jnp.int32
+    chunks = pltpu.VMEM((16, CAP, D), bf16)
+    counts = (2 * RING_SEMS, TABLE_SEMS + 16, 68)
     return pl.pallas_call(
-        attend_kernel,
+        layer_kernel,
         out_shape=(
+            jax.ShapeDtypeStruct((ROWS, 128), bf16),
             jax.ShapeDtypeStruct((ROWS, 64), bf16),
             jax.ShapeDtypeStruct((ROWS, 2 * HD), bf16),
         ),
-        in_specs=[vmem] * 2 + [far] * 4 + [vmem] * 4 + [far] * 2,
-        out_specs=(vmem, vmem),
+        in_specs=[far] * 3 + [vmem] * 3 + [far] * 3 + [vmem] * 2 + [far] * 4 + [vmem] * 3 + [far] * 2,
+        out_specs=(vmem,) * 3,
         scratch_shapes=[
+            pltpu.VMEM((ROWS, 2 * HD), bf16),
+            pltpu.VMEM((2 * HD, D), bf16),
+            pltpu.VMEM((ROWS, 128), bf16),
+            pltpu.VMEM((D, 384), bf16),
+            pltpu.VMEM((D, 384), bf16),
+            pltpu.VMEM((384, D), bf16),
+            pltpu.VMEM((D, 2 * HD), bf16),
+            pltpu.VMEM((D, 64), bf16),
+            pltpu.VMEM((ROWS, HD), f32),
+            pltpu.VMEM((ROWS, HD), f32),
+            pltpu.VMEM((8, 64, 4 * HD), bf16),
+            pltpu.VMEM((8, 64, 4 * HD), bf16),
+            pltpu.VMEM((8, 2, BLOCK, D), bf16),
+            pltpu.VMEM((8, 2, BLOCK, D), bf16),
+            pltpu.VMEM((BLOCK, D), bf16),
+            pltpu.VMEM((8, 128), i32),
+        ]
+        + ring_scratch()
+        + ring_scratch()
+        + [
+            chunks,
+            chunks,
+            chunks,
+            chunks,
+            pltpu.VMEM((16, CAP, HALF_D), bf16),
+            pltpu.VMEM((ROWS, D), f32),
+            pltpu.VMEM((16 * CAP, ROWS), bf16),
+            pltpu.VMEM((16, 8, 128), i32),
             pltpu.VMEM((ROWS, D), bf16),
             pltpu.VMEM((ROWS, 2 * HD), bf16),
             pltpu.VMEM((4, ROWS // 2, HD), bf16),
@@ -745,25 +737,14 @@
             pltpu.VMEM((16, 8, PACK), f32),
             pltpu.VMEM((8, PACK), f32),
             pltpu.VMEM((16, 8, PACK), f32),
-            pltpu.VMEM((D, 2 * HD), bf16),
-            pltpu.VMEM((D, 64), bf16),
-            pltpu.VMEM((ROWS, HD), f32),
-            pltpu.VMEM((ROWS, HD), f32),
-            pltpu.VMEM((8, 64, 4 * HD), bf16),
-            pltpu.VMEM((8, 64, 4 * HD), bf16),
-            pltpu.SemaphoreType.DMA((6,)),
-            pltpu.SemaphoreType.DMA((68,)),
-            pltpu.SemaphoreType.DMA((68,)),
-        ],
+            pltpu.SemaphoreType.DMA((12,)),
+        ]
+        + [pltpu.SemaphoreType.DMA((count,)) for count in counts for _ in range(2)],
         compiler_params=pltpu.CompilerParams(
-            collective_id=2, has_side_effects=True, vmem_limit_bytes=48 << 20
+            collective_id=0, has_side_effects=True, vmem_limit_bytes=60 << 20
         ),
-        name="attend",
-    )(
-        full, gain.reshape(1, D), w_query, w_keyval, cosine, sine,
-        segments.reshape(ROWS, 1), segments.reshape(1, ROWS), holders.reshape(8, 1), tables,
-        cache_keys, cache_values,
-    )
+        name="layer",
+    )(*operands)
 
 
 def shards(
@@ -800,15 +781,28 @@
     table = jnp.where(
         jnp.arange(128, dtype=jnp.int32)[None, :] // 8 == row, jnp.tile(table, (1, 16)), 0
     )
-    normed, mid = out_project(attn_context, w_out, residual, gain_post)
-    full, hidden_out, tables = experts(
-        normed.reshape(ROWS, D), routes.T, router_scores.T, w_gate[0], w_up[0], w_down[0], mid, table
-    )
-    new_cache, attention_out = attend(
-        full.reshape(ROWS, D), gain_input, w_query, w_keyval, cosine, sine, segments, holders, tables,
-        cache_keys, cache_values,
-    )
-    return (hidden_out, new_cache, attention_out)
+    return layer(
+        attn_context,
+        w_out,
+        residual,
+        gain_post.reshape(1, D),
+        routes.T,
+        router_scores.T,
+        w_gate[0],
+        w_up[0],
+        w_down[0],
+        table,
+        gain_input.reshape(1, D),
+        w_query,
+        w_keyval,
+        cosine,
+        sine,
+        segments.reshape(ROWS, 1),
+        segments.reshape(1, ROWS),
+        holders.reshape(8, 1),
+        cache_keys,
+        cache_values,
+    )
 
 
 def solution(mesh):

time: 236 us -> 222 us (0.941)
  Pallas kernels: 217 us -> 208 us
  local copies, waits for them, and re-layouts: 15.1 us -> 8.79 us
    unnamed x36 -> x17, local copies, waits for them, and re-layouts: 14 us -> 4.27 us
    pallas_call x3 -> x1, Pallas kernels: 217 us -> 208 us  [layer(): pl.pallas_call(layer_kernel, out_shape=(jax.ShapeDtypeStruct((ROWS, 128),...]
where the time goes in v4:
time: 222 us
  Pallas kernels  208 us (94%)
  local copies, waits for them, and re-layouts  8.79 us (4%)
  other arithmetic  4.4 us (2%)
    pallas_call x1, Pallas kernels, layer(): pl.pallas_call(layer_kernel, out_shape=(jax.ShapeDtypeStruct((ROWS, 128),...  208 us

profile of v4, /device:TPU:1, one launch (start us, length us, event | category | flops | bytes accessed | tf_op | source)
XLA Modules:
  0.0 222.2 jit_solution(13766700913044963406)
XLA Ops:
  0.6 0.0 copy-start.2
  0.6 0.0 copy-start
  0.7 1.1 convert_reduce_fusion
  1.7 0.7 add_convert_fusion
  2.5 0.0 copy-start.5
  2.5 0.0 copy-start.6
  2.5 0.0 copy-start.3
  2.5 0.0 copy-start.4
  2.5 1.0 fusion
  3.5 1.0 pad_maximum_fusion
  4.5 0.0 copy-done.2
  4.5 0.1 concatenate.19
  4.6 0.0 copy-start.1
  4.6 0.9 copy.28.segment_column
  5.4 0.0 copy-done
  5.4 1.0 copy.27.far_keyval
  6.4 0.0 copy-done.5
  6.4 0.0 copy-done.6
  6.5 0.1 tile.10
  6.6 0.6 broadcast_select_fusion.table
  7.2 0.0 copy-done.3
  7.2 0.6 reshape.86.gain_post
  7.8 0.0 copy-done.4
  7.8 0.6 reshape.87.gain_input
  8.4 0.7 copy.29.holders
  9.1 0.0 copy-done.1
  9.1 208.3 %layer.1 = (bf16[512,128]{1,0:T(8,128)(2,1)}, bf16[512,64]{1,0:T(8,128)(2,1)}, bf16[512,256]{1,0:T(8,128)(2,1)}) custom-call(bf16[512,256]{1,0:T(8,128)(2,1)} %far_context.1, bf16[256,2048]{1,0:T(8,128)(2,1)} %far_out.1, bf16[512,128]{1,0:T(8,128)(2,1)} %far_residual.1, bf16[1,2048]{1,0:T(2,128)(2,1)} %reshape.86.gain_post, s32[8,512]{1,0:T(8,128)} %bitcast.18, ...), custom_call_target="tpu_custom_call" | custom-call | tf_op jit(solution)/shard_map/layer/pallas_call | solution.py:689
  217.3 1.6 copy.30
  219.0 1.6 copy.33
  220.5 1.7 copy.34
  (6 shorter events, 0.0 us)
Async XLA Ops:
  0.6 3.9 %copy-start.2 = (s32[1,504]{1,0:T(1,128)S(1)}, s32[1,504]{1,0:T(1,128)}, u32[]{:S(2)}) copy-start(s32[1,504]{1,0:T(1,128)} %param.29) | copy-start | bytes 6052
  0.6 4.8 %copy-start = (bf16[2048,64]{0,1:T(8,128)(2,1)S(1)}, bf16[2048,64]{0,1:T(8,128)(2,1)}, u32[]{:S(2)}) copy-start(bf16[2048,64]{0,1:T(8,128)(2,1)} %param.28) | copy-start | bytes 786436
  2.5 4.0 %copy-start.5 = (s32[8]{0:T(128)S(1)}, s32[8]{0:T(128)}, u32[]{:S(2)}) copy-start(s32[8]{0:T(128)} %param.30) | copy-start | bytes 100
  2.5 4.0 %copy-start.6 = (s32[8]{0:T(128)S(1)}, s32[8]{0:T(128)}, u32[]{:S(2)}) copy-start(s32[8]{0:T(128)} %param.31) | copy-start | bytes 100
  2.5 4.7 %copy-start.3 = (bf16[2048]{0:T(1024)(128)(2,1)S(1)}, bf16[2048]{0:T(1024)(128)(2,1)}, u32[]{:S(2)}) copy-start(bf16[2048]{0:T(1024)(128)(2,1)} %param.20) | copy-start | bytes 12292
  2.5 5.3 %copy-start.4 = (bf16[2048]{0:T(1024)(128)(2,1)S(1)}, bf16[2048]{0:T(1024)(128)(2,1)}, u32[]{:S(2)}) copy-start(bf16[2048]{0:T(1024)(128)(2,1)} %param.21) | copy-start | bytes 12292
  4.6 4.5 %copy-start.1 = (s32[512]{0:T(512)}, s32[512]{0:T(512)S(1)}, u32[]{:S(2)}) copy-start(s32[512]{0:T(512)S(1)} %concatenate.19) | copy-start | bytes 6148

commit v5 on v4

--- a/solution.py
+++ b/solution.py
@@ -508,7 +508,9 @@
     asks = [go(own_query, all_query.at[row], o, along_row(o)) for o in range(1, 16)]
     for tile in range(0, ROWS, 64):
         x_in[tile : tile + 64, :] = norm(full[tile // 64].reshape(64, D))
-    keyval = jnp.dot(x_in[...], w_keyval[...], preferred_element_type=jnp.float32).astype(jnp.bfloat16)
+    keyval = lax.dot_general(
+        x_in[...], w_keyval[...], (((1,), (1,)), ((), ())), preferred_element_type=jnp.float32
+    ).astype(jnp.bfloat16)
     pieces[quarter] = jnp.concatenate([keyval[: ROWS // 2], keyval[ROWS // 2 :]], axis=1)
     shares = [
         go(pieces.at[quarter], pieces.at[quarter], 16 + o, (row, first + lax.rem(quarter + o, 4)))
@@ -648,12 +650,13 @@
 def layer_kernel(
     far_context, far_out, far_residual, gain_post, routes, scores, far_gate, far_up, far_down, table,
     gain_input, far_query, far_keyval, far_cosine, far_sine, segment_column, segment_row, holders,
-    far_keys, far_values, share, new_cache, attention, context, w_out, residual, w_gate, w_up, w_down,
+    far_keys, far_values, packed, context, w_out, residual, w_gate, w_up, w_down,
     w_query, w_keyval, cosine, sine, cache_keys, cache_values, normed, full, mid, tables, *rest,
 ):
     first_ring, second_ring, rest = rest[:7], rest[7:14], rest[14:]
     exchange, rest = rest[:8], rest[8:]
     heads, (fetched, *sems) = rest[:13], rest[13:]
+    share, attention, new_cache = packed.at[:, :128], packed.at[:, 128:384], packed.at[:, 384:448]
     near = (context, w_out, residual, w_gate, w_up, w_down)
     near = near + (w_query, w_keyval, cosine, sine, cache_keys, cache_values)
     far = (far_context, far_out, far_residual, far_gate, far_up, far_down)
@@ -688,13 +691,9 @@
     counts = (2 * RING_SEMS, TABLE_SEMS + 16, 68)
     return pl.pallas_call(
         layer_kernel,
-        out_shape=(
-            jax.ShapeDtypeStruct((ROWS, 128), bf16),
-            jax.ShapeDtypeStruct((ROWS, 64), bf16),
-            jax.ShapeDtypeStruct((ROWS, 2 * HD), bf16),
-        ),
+        out_shape=jax.ShapeDtypeStruct((ROWS, 512), bf16),
         in_specs=[far] * 3 + [vmem] * 3 + [far] * 3 + [vmem] * 2 + [far] * 4 + [vmem] * 3 + [far] * 2,
-        out_specs=(vmem,) * 3,
+        out_specs=vmem,
         scratch_shapes=[
             pltpu.VMEM((ROWS, 2 * HD), bf16),
             pltpu.VMEM((2 * HD, D), bf16),
@@ -703,7 +702,7 @@
             pltpu.VMEM((D, 384), bf16),
             pltpu.VMEM((384, D), bf16),
             pltpu.VMEM((D, 2 * HD), bf16),
-            pltpu.VMEM((D, 64), bf16),
+            pltpu.VMEM((64, D), bf16),
             pltpu.VMEM((ROWS, HD), f32),
             pltpu.VMEM((ROWS, HD), f32),
             pltpu.VMEM((8, 64, 4 * HD), bf16),
@@ -781,7 +780,7 @@
     table = jnp.where(
         jnp.arange(128, dtype=jnp.int32)[None, :] // 8 == row, jnp.tile(table, (1, 16)), 0
     )
-    return layer(
+    packed = layer(
         attn_context,
         w_out,
         residual,
@@ -794,7 +793,7 @@
         table,
         gain_input.reshape(1, D),
         w_query,
-        w_keyval,
+        w_keyval.T,
         cosine,
         sine,
         segments.reshape(ROWS, 1),
@@ -803,6 +802,7 @@
         cache_keys,
         cache_values,
     )
+    return (packed[:, :128], packed[:, 384:448], packed[:, 128:384])
 
 
 def solution(mesh):

time: 222 us -> 222 us (level)
    slice x0 -> x3, local copies, waits for them, and re-layouts: none -> 4.15 us  [shards(): return (packed[:, :128], packed[:, 384:448], packed[:, 128:384])]
    unnamed x17 -> x13, local copies, waits for them, and re-layouts: 4.27 us -> 0.76 us
where the time goes in v5:
time: 222 us; the launch traced here: 221 us
  Pallas kernels  208 us (94%)
  local copies, waits for them, and re-layouts  7.82 us (4%)
  other arithmetic  4.36 us (2%)
    pallas_call x1, Pallas kernels, layer(): pl.pallas_call(layer_kernel, out_shape=jax.ShapeDtypeStruct((ROWS, 512),...  208 us

profile of v5, /device:TPU:1, one launch (start us, length us, event | category | flops | bytes accessed | tf_op | source)
XLA Modules:
  0.0 221.4 jit_solution(15437069331760050720)
XLA Ops:
  0.6 0.0 copy-start.1
  0.6 0.0 copy-start.4
  0.7 0.0 copy-start.5
  0.7 0.0 copy-start.2
  0.7 0.0 copy-start.3
  0.7 1.0 convert_reduce_fusion
  1.7 0.7 add_convert_fusion
  2.5 1.0 fusion
  3.5 1.0 pad_maximum_fusion
  4.5 0.0 copy-done.1
  4.5 0.1 concatenate.19
  4.5 0.0 copy-start
  4.5 0.9 copy.25.segment_column
  5.4 0.0 copy-done.4
  5.4 0.0 copy-done.5
  5.4 0.1 tile.10
  5.5 0.6 broadcast_select_fusion.table
  6.1 0.0 copy-done.2
  6.1 0.6 reshape.86.gain_post
  6.7 0.0 copy-done.3
  6.7 0.6 reshape.87.gain_input
  7.4 0.7 copy.26.holders
  8.0 0.0 copy-done
  8.0 208.5 %layer.1 = bf16[512,512]{1,0:T(8,128)(2,1)} custom-call(bf16[512,256]{1,0:T(8,128)(2,1)} %far_context.1, bf16[256,2048]{1,0:T(8,128)(2,1)} %far_out.1, bf16[512,128]{1,0:T(8,128)(2,1)} %far_residual.1, bf16[1,2048]{1,0:T(2,128)(2,1)} %reshape.86.gain_post, s32[8,512]{1,0:T(8,128)} %bitcast.20, f32[8,512]{1,0:T(8,128)} %bitcast.21, ...), custom_call_target="tpu_custom_call" | custom-call | tf_op jit(solution)/shard_map/layer/pallas_call | solution.py:692
  216.5 1.7 slice.11
  218.2 0.9 slice.10
  219.1 0.7 copy.27
  219.8 1.6 slice.9
  (6 shorter events, 0.0 us)
Async XLA Ops:
  0.6 3.8 %copy-start.1 = (s32[1,504]{1,0:T(1,128)S(1)}, s32[1,504]{1,0:T(1,128)}, u32[]{:S(2)}) copy-start(s32[1,504]{1,0:T(1,128)} %param.29) | copy-start | bytes 6052
  0.6 4.8 %copy-start.4 = (s32[8]{0:T(128)S(1)}, s32[8]{0:T(128)}, u32[]{:S(2)}) copy-start(s32[8]{0:T(128)} %param.30) | copy-start | bytes 100
  0.7 4.7 %copy-start.5 = (s32[8]{0:T(128)S(1)}, s32[8]{0:T(128)}, u32[]{:S(2)}) copy-start(s32[8]{0:T(128)} %param.31) | copy-start | bytes 100
  0.7 5.5 %copy-start.2 = (bf16[2048]{0:T(1024)(128)(2,1)S(1)}, bf16[2048]{0:T(1024)(128)(2,1)}, u32[]{:S(2)}) copy-start(bf16[2048]{0:T(1024)(128)(2,1)} %param.20) | copy-start | bytes 12292
  0.7 6.1 %copy-start.3 = (bf16[2048]{0:T(1024)(128)(2,1)S(1)}, bf16[2048]{0:T(1024)(128)(2,1)}, u32[]{:S(2)}) copy-start(bf16[2048]{0:T(1024)(128)(2,1)} %param.21) | copy-start | bytes 12292
  4.5 3.5 %copy-start = (s32[512]{0:T(512)}, s32[512]{0:T(512)S(1)}, u32[]{:S(2)}) copy-start(s32[512]{0:T(512)S(1)} %concatenate.19) | copy-start | bytes 6148
